TPU v7x, 768 devices: a whole 4x8x12 slice. The times are simulated.
768 devices in a mesh: section: 8 (over y), shard: 96 (over z, x, core).
Axes of the slice: x: 4, y: 8, z: 12, core: 2. Of those that a mesh axis runs over, the one named last changes fastest.
Arguments:
- features: bfloat16 [2, 96, 64, 1536], P(None, 'shard'), may hold values from -6 to 6
- window_building_index: int32 [2, 96], P(None, 'shard'), may hold values from 0 to 127
- building_embeddings: bfloat16 [128, 1536], replicated, may hold values from -6 to 6
- dilation_exponent: int32 [8], P('section'), may hold values from 0 to 5
- weights: bfloat16 [8, 2, 1536, 1536], P('section', None, 'shard'), may hold values from -0.109375 to 0.109375
- cotangent: bfloat16 [2, 96, 64, 1536], P(None, 'shard'), may hold values from -0.053955078 to 0.053955078
Outputs:
- grad_weights: float32 [8, 2, 1536, 1536], P('section', None, 'shard')
All inputs are finite; a program needn't handle non-finite values.
Results may differ from a plain program's by a relative error of at most 0.017.
Values may be sent and summed in bfloat16 or wider, within the bound.
No kernel may reach another device: no remote copies, remote signals or barrier semaphores. Data moves between devices by JAX's collectives and lax.ppermute only.
A program may use at most 128 MiB of HBM per device.

v0:
```python
import jax
import jax.numpy as jnp
from jax import lax
from jax.sharding import PartitionSpec as P


def from_behind(block, axis, distance):
    devices = range(lax.axis_size(axis))
    route = [(i - distance, i) for i in devices if i - distance in devices]
    return lax.ppermute(block, axis, route)


def delayed(values, time_offset):
    length = values.shape[-2]
    padded = jnp.concatenate([jnp.zeros_like(values), values], axis=-2)
    return lax.dynamic_slice_in_dim(padded, length - time_offset, length, axis=values.ndim - 2)


def advanced(values, time_offset):
    length = values.shape[-2]
    padded = jnp.concatenate([values, jnp.zeros_like(values)], axis=-2)
    return lax.dynamic_slice_in_dim(padded, time_offset, length, axis=values.ndim - 2)


def prepare(x_in, time_offset):
    width = x_in.shape[-1]
    x_full = x_in.astype(jnp.float32)
    inverse = lax.rsqrt(jnp.mean(x_full * x_full, axis=-1, keepdims=True) + 1e-06)
    normed = x_full * inverse
    rounded = normed.astype(jnp.bfloat16)
    both = jnp.concatenate([rounded, delayed(rounded, time_offset)], axis=-1).reshape(-1, 2 * width)
    return (x_full, inverse, normed, both)


def layer_forward(x_in, w_flat, time_offset):
    x_full, inverse, normed, both = prepare(x_in, time_offset)
    pre = jnp.dot(both, w_flat, preferred_element_type=jnp.float32).reshape(x_in.shape)
    return (x_full + jax.nn.silu(pre)).astype(jnp.bfloat16)


def layer_parts(x_in, upstream, w_flat, time_offset):
    width = x_in.shape[-1]
    x_full, inverse, normed, both = prepare(x_in, time_offset)
    pre = jnp.dot(both, w_flat, preferred_element_type=jnp.float32).reshape(x_in.shape)
    grad_up = upstream.astype(jnp.float32)
    sigma = jax.nn.sigmoid(pre)
    d_pre = (grad_up * sigma * (1.0 + pre * (1.0 - sigma))).astype(jnp.bfloat16).reshape(-1, width)
    back = lax.dot_general(
        d_pre, w_flat, (((1,), (1,)), ((), ())), preferred_element_type=jnp.float32
    )
    back = back.reshape(x_in.shape[:-1] + (2 * width,))
    d_norm = back[..., :width] + advanced(back[..., width:], time_offset)
    d_x = grad_up + inverse * (d_norm - normed * jnp.mean(d_norm * normed, axis=-1, keepdims=True))
    return (d_x.astype(jnp.bfloat16), both, d_pre)


def pass_back(values):
    return from_behind(values, "section", -1)


def shards(
    features, window_building_index, building_embeddings, dilation_exponent, weights, cotangent
):
    sections = lax.axis_size("section")
    here = lax.axis_index("section")
    micro = features.shape[0]
    width = features.shape[3]
    time_offset = jnp.left_shift(jnp.ones_like(dilation_exponent[0]), dilation_exponent[0])
    onehot = (
        window_building_index[:, :, None]
        == jnp.arange(building_embeddings.shape[0], dtype=jnp.int32)[None, None, :]
    ).astype(jnp.bfloat16)
    bias = jnp.einsum(
        "mwb,bc->mwc", onehot, building_embeddings, preferred_element_type=jnp.float32
    )
    inputs = (features.astype(jnp.float32) + bias[:, :, None, :]).astype(jnp.bfloat16)
    gathered = lax.all_gather(weights[0], "shard", axis=1, tiled=True)
    w_flat = gathered.reshape(2 * width, width)
    ticks = sections + micro - 1
    block = inputs[0]

    def forward_tick(tick, carry):
        incoming, store = carry
        index = tick - here
        valid = jnp.logical_and(index >= 0, index < micro)
        slot = jnp.clip(index, 0, micro - 1)
        own = lax.dynamic_index_in_dim(inputs, slot, 0, keepdims=False)
        source = jnp.where(here == 0, own, incoming)
        store = lax.cond(
            valid,
            lambda kept: lax.dynamic_update_index_in_dim(kept, source, slot, 0),
            lambda kept: kept,
            store,
        )
        result = lax.cond(
            valid,
            lambda value: layer_forward(value, w_flat, time_offset),
            lambda value: value,
            source,
        )
        incoming = from_behind(result, "section", 1)
        return (incoming, store)

    first, store = lax.fori_loop(
        0, ticks, forward_tick, (jnp.zeros_like(block), jnp.zeros_like(inputs))
    )

    def tick_inputs(tick, incoming):
        index = tick - (sections - 1 - here)
        valid = jnp.logical_and(index >= 0, index < micro)
        slot = jnp.clip(index, 0, micro - 1)
        own = lax.dynamic_index_in_dim(cotangent, slot, 0, keepdims=False)
        upstream = jnp.where(here == sections - 1, own, incoming)
        saved = lax.dynamic_index_in_dim(store, slot, 0, keepdims=False)
        return (valid, slot, upstream, saved)

    def backward_tick(tick, carry):
        incoming, total = carry
        valid, slot, upstream, saved = tick_inputs(tick, incoming)

        def run(summed):
            d_x, both, d_pre = layer_parts(saved, upstream, w_flat, time_offset)
            grad_w = lax.dot_general(
                both, d_pre, (((0,), (0,)), ((), ())), preferred_element_type=jnp.float32
            )
            return (d_x, summed + grad_w)

        def skip(summed):
            return (jnp.zeros_like(upstream), summed)

        d_x, total = lax.cond(valid, run, skip, total)
        incoming = pass_back(d_x)
        return (incoming, total)

    empty = jnp.zeros((2 * width, width), jnp.float32)
    last, total = lax.fori_loop(0, ticks, backward_tick, (jnp.zeros_like(block), empty))
    owned = lax.psum_scatter(
        total.reshape(2, width, width), "shard", scatter_dimension=1, tiled=True
    )
    return owned[None]


def solution(mesh):
    placed = (
        P(None, "shard", None, None),
        P(None, "shard"),
        P(),
        P("section"),
        P("section", None, "shard", None),
        P(None, "shard", None, None),
    )
    return jax.shard_map(
        shards,
        mesh=mesh,
        in_specs=placed,
        out_specs=P("section", None, "shard", None),
        check_vma=False,
    )
```

profile of v0, /device:TPU:8, one launch (start us, length us, event | category | flops | bytes accessed | tf_op | source)
XLA Modules:
  0.0 797.6 jit_solution(7479924975061523413)
XLA Ops:
  6.5 0.7 all-gather.3.cloned.1.call-update
  8.0 0.9 fusion.22
  8.8 1.1 add_convert_fusion
  9.9 132.3 %all-gather.3.cloned.1.call-done = bf16[1,2,1536,1536]{3,2,1,0:T(8,128)(2,1)} async-done(((bf16[1,2,16,1536]{3,2,1,0:T(8,128)(2,1)}), bf16[1,2,1536,1536]{3,2,1,0:T(8,128)(2,1)}) %all-gather.3.cloned.1.call-update) | async-done | bytes 9437200 | tf_op jit(solution)/shard_map/all_gather | solution.py:77
  142.2 101.5 %while.39 = (s32[]{:T(128)}, bf16[1,64,1536]{2,1,0:T(8,128)(2,1)S(1)}, bf16[2,1,64,1536]{3,2,1,0:T(8,128)(2,1)S(1)}, s32[]{:T(128)}, pred[]{:T(512)}, /*index=5*...) while((s32[]{:T(128)}, ...), condition=%wide.region_6.7_spmd, body=%wide.region_0.6_spmd.sunk | while | flops 606142528 | bytes 12977520 | solution.py:104
  142.4 3.4 collective-permute-start
  145.8 9.6 %collective-permute-done = bf16[1,64,1536]{2,1,0:T(8,128)(2,1)S(1)} collective-permute-done((bf16[1,64,1536]{2,1,0:T(8,128)(2,1)S(1)}, bf16[1,64,1536]{2,1,0:T(8,128)(2,1)S(1)}, u32[]{:S(2)}, u32[]{:S(2)}) %collective-permute-start) | collective-permute-done | bytes 196640 | tf_op jit(solution)/shard_map/while/body/eval_jaxpr/ppermute | solution.py:10
  155.4 5.9 conditional.6
  155.4 0.1 fusion
  155.8 5.5 fusion.2
  161.3 1.9 collective-permute-start
  163.3 6.5 collective-permute-done
  169.8 5.9 conditional.6
  169.8 0.1 fusion
  170.2 5.5 fusion.2
  175.7 2.2 collective-permute-start
  177.9 5.3 collective-permute-done
  183.3 8.4 %collective-permute-start = (bf16[1,64,1536]{2,1,0:T(8,128)(2,1)S(1)}, bf16[1,64,1536]{2,1,0:T(8,128)(2,1)S(1)}, u32[]{:S(2)}, u32[]{:S(2)}) collective-permute-start(bf16[1,64,1536]{2,1,0:T(8,128)(2,1)S(1)} %get-tuple-element.691), channel_id=1, source_target_pairs={{0,96},{96,192},{192,288},{288,384},{384,480},{480,576},{576,672},... | collective-permute-start | bytes 589832 | tf_op jit(solution)/shard_map/while/body/eval_jaxpr/ppermute | solution.py:10
  191.7 3.1 collective-permute-done
  195.0 4.4 collective-permute-start
  199.4 3.1 collective-permute-done
  202.6 8.1 %collective-permute-start = (bf16[1,64,1536]{2,1,0:T(8,128)(2,1)S(1)}, bf16[1,64,1536]{2,1,0:T(8,128)(2,1)S(1)}, u32[]{:S(2)}, u32[]{:S(2)}) collective-permute-start(bf16[1,64,1536]{2,1,0:T(8,128)(2,1)S(1)} %get-tuple-element.691), channel_id=1, source_target_pairs={{0,96},{96,192},{192,288},{288,384},{384,480},{480,576},{576,672},... | collective-permute-start | bytes 589832 | tf_op jit(solution)/shard_map/while/body/eval_jaxpr/ppermute | solution.py:10
  210.7 3.1 collective-permute-done
  213.9 4.4 collective-permute-start
  218.3 4.0 collective-permute-done
  222.3 9.4 %collective-permute-start = (bf16[1,64,1536]{2,1,0:T(8,128)(2,1)S(1)}, bf16[1,64,1536]{2,1,0:T(8,128)(2,1)S(1)}, u32[]{:S(2)}, u32[]{:S(2)}) collective-permute-start(bf16[1,64,1536]{2,1,0:T(8,128)(2,1)S(1)} %get-tuple-element.691), channel_id=1, source_target_pairs={{0,96},{96,192},{192,288},{288,384},{384,480},{480,576},{576,672},... | collective-permute-start | bytes 589832 | tf_op jit(solution)/shard_map/while/body/eval_jaxpr/ppermute | solution.py:10
  231.8 3.6 collective-permute-done
  235.5 5.1 collective-permute-start
  240.6 3.1 collective-permute-done
  243.8 8.9 %broadcast_in_dim.13 = f32[3072,1536]{1,0:T(8,128)} broadcast(f32[]{:T(128)} %constant.160.clone.1), dimensions={} | broadcast | bytes 18874372 | tf_op jit(solution)/shard_map/broadcast_in_dim | solution.py:135
  252.7 282.7 %while.40 = (s32[]{:T(128)}, bf16[1,64,1536]{2,1,0:T(8,128)(2,1)S(1)}, f32[3072,1536]{1,0:T(8,128)}, s32[]{:T(128)}, pred[]{:T(512)}, /*index=5*/bf16[2,1,64,153...) while((s32[]{:T(128)}, ...), condition=%wide.region_12.13_spmd, body=%wide.region_7.12_spmd.sunk | while | flops 1821376512 | bytes 92605408 | solution.py:136
  252.7 1.9 collective-permute-start.1
  254.7 12.4 %collective-permute-done.1 = bf16[1,64,1536]{2,1,0:T(8,128)(2,1)S(1)} collective-permute-done((bf16[1,64,1536]{2,1,0:T(8,128)(2,1)S(1)}, bf16[1,64,1536]{2,1,0:T(8,128)(2,1)S(1)}, u32[]{:S(2)}, u32[]{:S(2)}) %collective-permute-start.1) | collective-permute-done | bytes 196640 | tf_op jit(solution)/shard_map/while/body/eval_jaxpr/ppermute | solution.py:10
  267.1 1.9 collective-permute-start.1
  269.0 8.0 %collective-permute-done.1 = bf16[1,64,1536]{2,1,0:T(8,128)(2,1)S(1)} collective-permute-done((bf16[1,64,1536]{2,1,0:T(8,128)(2,1)S(1)}, bf16[1,64,1536]{2,1,0:T(8,128)(2,1)S(1)}, u32[]{:S(2)}, u32[]{:S(2)}) %collective-permute-start.1) | collective-permute-done | bytes 196640 | tf_op jit(solution)/shard_map/while/body/eval_jaxpr/ppermute | solution.py:10
  277.1 1.9 collective-permute-start.1
  279.0 7.8 collective-permute-done.1
  286.8 1.9 collective-permute-start.1
  288.8 7.6 collective-permute-done.1
  296.4 1.9 collective-permute-start.1
  298.3 6.2 collective-permute-done.1
  304.5 1.9 collective-permute-start.1
  306.5 139.2 %collective-permute-done.1 = bf16[1,64,1536]{2,1,0:T(8,128)(2,1)S(1)} collective-permute-done((bf16[1,64,1536]{2,1,0:T(8,128)(2,1)S(1)}, bf16[1,64,1536]{2,1,0:T(8,128)(2,1)S(1)}, u32[]{:S(2)}, u32[]{:S(2)}) %collective-permute-start.1) | collective-permute-done | bytes 196640 | tf_op jit(solution)/shard_map/while/body/eval_jaxpr/ppermute | solution.py:10
  445.7 22.7 %conditional.8 = (bf16[1,64,1536]{2,1,0:T(8,128)(2,1)S(1)}, f32[3072,1536]{1,0:T(8,128)}) conditional(s32[]{:T(128)} %convert_element_type.120, f32[3072,1536]{1,0:T(8,128)} %get-tuple-element.669, (pred[]{:T(512)}, s32[]{:T(128)}, bf16[2,1,64,1536]{3,2,1,0:T(8,128)(2,1)S(1)}, bf16[1,64,1536]{2,1,0:T(8,128)(2,1)S(1)}, ...), branch_computations={%region_8.8_spmd, %region_9.11_spmd} | conditional | flops 1821376512 | bytes 91818720 | solution.py:131
  445.7 0.1 fusion.16
  446.1 5.7 fusion.19
  451.8 13.2 %convolution_add_fusion = f32[3072,1536]{1,0:T(8,128)} fusion(f32[3072,1536]{1,0:T(8,128)} %get-tuple-element.459, bf16[64,1536]{1,0:T(8,128)(2,1)S(1)} %fusion.19, bf16[1,64,1536]{2,1,0:T(8,128)(2,1)S(1)} %pad_dynamic-slice_fusion.2, bf16[1,64,1536]{2,1,0:T(8,128)(2,1)S(1)} %fusion.9), kind=kOutput, calls=%fused_computation.15 | convolution fusion | flops 609484800 | bytes 38338560 | tf_op jit(solution)/shard_map/while/body/eval_jaxpr/cond/branch_1_fun/dot_general | solution.py:123
  465.0 2.9 convolution_bitcast_fusion
  468.0 0.2 fusion.13
  468.2 0.2 fusion.12
  468.4 1.9 collective-permute-start.1
  470.4 6.8 collective-permute-done.1
  477.2 22.7 %conditional.8 = (bf16[1,64,1536]{2,1,0:T(8,128)(2,1)S(1)}, f32[3072,1536]{1,0:T(8,128)}) conditional(s32[]{:T(128)} %convert_element_type.120, f32[3072,1536]{1,0:T(8,128)} %get-tuple-element.669, (pred[]{:T(512)}, s32[]{:T(128)}, bf16[2,1,64,1536]{3,2,1,0:T(8,128)(2,1)S(1)}, bf16[1,64,1536]{2,1,0:T(8,128)(2,1)S(1)}, ...), branch_computations={%region_8.8_spmd, %region_9.11_spmd} | conditional | flops 1821376512 | bytes 91818720 | solution.py:131
  477.2 0.1 fusion.16
  477.6 5.7 fusion.19
  483.3 13.2 %convolution_add_fusion = f32[3072,1536]{1,0:T(8,128)} fusion(f32[3072,1536]{1,0:T(8,128)} %get-tuple-element.459, bf16[64,1536]{1,0:T(8,128)(2,1)S(1)} %fusion.19, bf16[1,64,1536]{2,1,0:T(8,128)(2,1)S(1)} %pad_dynamic-slice_fusion.2, bf16[1,64,1536]{2,1,0:T(8,128)(2,1)S(1)} %fusion.9), kind=kOutput, calls=%fused_computation.15 | convolution fusion | flops 609484800 | bytes 38338560 | tf_op jit(solution)/shard_map/while/body/eval_jaxpr/cond/branch_1_fun/dot_general | solution.py:123
  496.5 2.9 convolution_bitcast_fusion
  499.5 0.2 fusion.13
  499.7 0.2 fusion.12
  499.9 1.9 collective-permute-start.1
  501.9 5.6 collective-permute-done.1
  507.5 24.6 %collective-permute-start.1 = (bf16[1,64,1536]{2,1,0:T(8,128)(2,1)S(1)}, bf16[1,64,1536]{2,1,0:T(8,128)(2,1)S(1)}, u32[]{:S(2)}, u32[]{:S(2)}) collective-permute-start(bf16[1,64,1536]{2,1,0:T(8,128)(2,1)S(1)} %get-tuple-element.616), channel_id=1, source_target_pairs={{96,0},{192,96},{288,192},{384,288},{480,384},{576,480},{672,576},... | collective-permute-start | bytes 589832 | tf_op jit(solution)/shard_map/while/body/eval_jaxpr/ppermute | solution.py:10
  532.2 3.2 collective-permute-done.1
  535.3 255.4 %reduce-scatter.2.cloned.1.call-done = f32[2,16,1536]{2,1,0:T(8,128)} async-done(((f32[2,1536,1536]{2,1,0:T(8,128)}), f32[2,16,1536]{2,1,0:T(8,128)}) %reduce-scatter.2.cloned.1.call-update) | async-done | bytes 196624 | tf_op jit(solution)/shard_map/reduce_scatter | solution.py:137
  (88 shorter events, 2.1 us)
Async XLA Ops:
  6.5 1.4 copy-start
  6.5 135.7 %all-gather.3.cloned.1.call-start = ((), (), s32[]{:S(2)}) async-start(), calls=%async_computation.2 | async-start | bytes 9535488 | tf_op jit(solution)/shard_map/all_gather | solution.py:77
  7.3 783.5 %reduce-scatter.2.cloned.1.call-start = ((), (), s32[]{:S(2)}) async-start(), calls=%async_computation.1 | async-start | bytes 19070976 | tf_op jit(solution)/shard_map/reduce_scatter | solution.py:137
  142.4 13.0 %collective-permute-start = (bf16[1,64,1536]{2,1,0:T(8,128)(2,1)S(1)}, bf16[1,64,1536]{2,1,0:T(8,128)(2,1)S(1)}, u32[]{:S(2)}, u32[]{:S(2)}) collective-permute-start(bf16[1,64,1536]{2,1,0:T(8,128)(2,1)S(1)} %get-tuple-element.691), channel_id=1, source_target_pairs={{0,96},{96,192},{192,288},{288,384},{384,480},{480,576},{576,672},... | collective-permute-start | bytes 589832 | tf_op jit(solution)/shard_map/while/body/eval_jaxpr/ppermute | solution.py:10
  161.3 8.5 %collective-permute-start = (bf16[1,64,1536]{2,1,0:T(8,128)(2,1)S(1)}, bf16[1,64,1536]{2,1,0:T(8,128)(2,1)S(1)}, u32[]{:S(2)}, u32[]{:S(2)}) collective-permute-start(bf16[1,64,1536]{2,1,0:T(8,128)(2,1)S(1)} %get-tuple-element.691), channel_id=1, source_target_pairs={{0,96},{96,192},{192,288},{288,384},{384,480},{480,576},{576,672},... | collective-permute-start | bytes 589832 | tf_op jit(solution)/shard_map/while/body/eval_jaxpr/ppermute | solution.py:10
  175.7 7.6 collective-permute-start
  183.3 11.6 %collective-permute-start = (bf16[1,64,1536]{2,1,0:T(8,128)(2,1)S(1)}, bf16[1,64,1536]{2,1,0:T(8,128)(2,1)S(1)}, u32[]{:S(2)}, u32[]{:S(2)}) collective-permute-start(bf16[1,64,1536]{2,1,0:T(8,128)(2,1)S(1)} %get-tuple-element.691), channel_id=1, source_target_pairs={{0,96},{96,192},{192,288},{288,384},{384,480},{480,576},{576,672},... | collective-permute-start | bytes 589832 | tf_op jit(solution)/shard_map/while/body/eval_jaxpr/ppermute | solution.py:10
  195.0 7.6 collective-permute-start
  202.6 11.2 %collective-permute-start = (bf16[1,64,1536]{2,1,0:T(8,128)(2,1)S(1)}, bf16[1,64,1536]{2,1,0:T(8,128)(2,1)S(1)}, u32[]{:S(2)}, u32[]{:S(2)}) collective-permute-start(bf16[1,64,1536]{2,1,0:T(8,128)(2,1)S(1)} %get-tuple-element.691), channel_id=1, source_target_pairs={{0,96},{96,192},{192,288},{288,384},{384,480},{480,576},{576,672},... | collective-permute-start | bytes 589832 | tf_op jit(solution)/shard_map/while/body/eval_jaxpr/ppermute | solution.py:10
  213.9 8.4 %collective-permute-start = (bf16[1,64,1536]{2,1,0:T(8,128)(2,1)S(1)}, bf16[1,64,1536]{2,1,0:T(8,128)(2,1)S(1)}, u32[]{:S(2)}, u32[]{:S(2)}) collective-permute-start(bf16[1,64,1536]{2,1,0:T(8,128)(2,1)S(1)} %get-tuple-element.691), channel_id=1, source_target_pairs={{0,96},{96,192},{192,288},{288,384},{384,480},{480,576},{576,672},... | collective-permute-start | bytes 589832 | tf_op jit(solution)/shard_map/while/body/eval_jaxpr/ppermute | solution.py:10
  222.3 13.0 %collective-permute-start = (bf16[1,64,1536]{2,1,0:T(8,128)(2,1)S(1)}, bf16[1,64,1536]{2,1,0:T(8,128)(2,1)S(1)}, u32[]{:S(2)}, u32[]{:S(2)}) collective-permute-start(bf16[1,64,1536]{2,1,0:T(8,128)(2,1)S(1)} %get-tuple-element.691), channel_id=1, source_target_pairs={{0,96},{96,192},{192,288},{288,384},{384,480},{480,576},{576,672},... | collective-permute-start | bytes 589832 | tf_op jit(solution)/shard_map/while/body/eval_jaxpr/ppermute | solution.py:10
  235.5 8.3 %collective-permute-start = (bf16[1,64,1536]{2,1,0:T(8,128)(2,1)S(1)}, bf16[1,64,1536]{2,1,0:T(8,128)(2,1)S(1)}, u32[]{:S(2)}, u32[]{:S(2)}) collective-permute-start(bf16[1,64,1536]{2,1,0:T(8,128)(2,1)S(1)} %get-tuple-element.691), channel_id=1, source_target_pairs={{0,96},{96,192},{192,288},{288,384},{384,480},{480,576},{576,672},... | collective-permute-start | bytes 589832 | tf_op jit(solution)/shard_map/while/body/eval_jaxpr/ppermute | solution.py:10
  243.8 8.9 %copy-start.1 = (bf16[2,1,64,1536]{3,2,1,0:T(8,128)(2,1)S(1)}, bf16[2,1,64,1536]{3,2,1,0:T(8,128)(2,1)}, u32[]{:S(2)}) copy-start(bf16[2,1,64,1536]{3,2,1,0:T(8,128)(2,1)} %param.21) | copy-start | bytes 1179652
  252.7 14.3 %collective-permute-start.1 = (bf16[1,64,1536]{2,1,0:T(8,128)(2,1)S(1)}, bf16[1,64,1536]{2,1,0:T(8,128)(2,1)S(1)}, u32[]{:S(2)}, u32[]{:S(2)}) collective-permute-start(bf16[1,64,1536]{2,1,0:T(8,128)(2,1)S(1)} %get-tuple-element.616), channel_id=1, source_target_pairs={{96,0},{192,96},{288,192},{384,288},{480,384},{576,480},{672,576},... | collective-permute-start | bytes 589832 | tf_op jit(solution)/shard_map/while/body/eval_jaxpr/ppermute | solution.py:10
  267.1 9.9 %collective-permute-start.1 = (bf16[1,64,1536]{2,1,0:T(8,128)(2,1)S(1)}, bf16[1,64,1536]{2,1,0:T(8,128)(2,1)S(1)}, u32[]{:S(2)}, u32[]{:S(2)}) collective-permute-start(bf16[1,64,1536]{2,1,0:T(8,128)(2,1)S(1)} %get-tuple-element.616), channel_id=1, source_target_pairs={{96,0},{192,96},{288,192},{384,288},{480,384},{576,480},{672,576},... | collective-permute-start | bytes 589832 | tf_op jit(solution)/shard_map/while/body/eval_jaxpr/ppermute | solution.py:10
  277.1 9.7 %collective-permute-start.1 = (bf16[1,64,1536]{2,1,0:T(8,128)(2,1)S(1)}, bf16[1,64,1536]{2,1,0:T(8,128)(2,1)S(1)}, u32[]{:S(2)}, u32[]{:S(2)}) collective-permute-start(bf16[1,64,1536]{2,1,0:T(8,128)(2,1)S(1)} %get-tuple-element.616), channel_id=1, source_target_pairs={{96,0},{192,96},{288,192},{384,288},{480,384},{576,480},{672,576},... | collective-permute-start | bytes 589832 | tf_op jit(solution)/shard_map/while/body/eval_jaxpr/ppermute | solution.py:10
  286.8 9.5 %collective-permute-start.1 = (bf16[1,64,1536]{2,1,0:T(8,128)(2,1)S(1)}, bf16[1,64,1536]{2,1,0:T(8,128)(2,1)S(1)}, u32[]{:S(2)}, u32[]{:S(2)}) collective-permute-start(bf16[1,64,1536]{2,1,0:T(8,128)(2,1)S(1)} %get-tuple-element.616), channel_id=1, source_target_pairs={{96,0},{192,96},{288,192},{384,288},{480,384},{576,480},{672,576},... | collective-permute-start | bytes 589832 | tf_op jit(solution)/shard_map/while/body/eval_jaxpr/ppermute | solution.py:10
  296.4 8.1 %collective-permute-start.1 = (bf16[1,64,1536]{2,1,0:T(8,128)(2,1)S(1)}, bf16[1,64,1536]{2,1,0:T(8,128)(2,1)S(1)}, u32[]{:S(2)}, u32[]{:S(2)}) collective-permute-start(bf16[1,64,1536]{2,1,0:T(8,128)(2,1)S(1)} %get-tuple-element.616), channel_id=1, source_target_pairs={{96,0},{192,96},{288,192},{384,288},{480,384},{576,480},{672,576},... | collective-permute-start | bytes 589832 | tf_op jit(solution)/shard_map/while/body/eval_jaxpr/ppermute | solution.py:10
  304.5 141.1 %collective-permute-start.1 = (bf16[1,64,1536]{2,1,0:T(8,128)(2,1)S(1)}, bf16[1,64,1536]{2,1,0:T(8,128)(2,1)S(1)}, u32[]{:S(2)}, u32[]{:S(2)}) collective-permute-start(bf16[1,64,1536]{2,1,0:T(8,128)(2,1)S(1)} %get-tuple-element.616), channel_id=1, source_target_pairs={{96,0},{192,96},{288,192},{384,288},{480,384},{576,480},{672,576},... | collective-permute-start | bytes 589832 | tf_op jit(solution)/shard_map/while/body/eval_jaxpr/ppermute | solution.py:10
  446.0 18.9 %slice-start = ((s8[9437184]{0:T(1024)(128)(4,1)}), s8[4194304]{0:T(1024)(128)(4,1)S(1)}, s32[]{:S(2)}) async-start(s8[9437184]{0:T(1024)(128)(4,1)} %bitcast.57), calls=%async_computation.3 | async-start | bytes 8388608 | tf_op jit(solution)/shard_map/while/body/eval_jaxpr/cond
  451.7 13.3 %slice-start.1 = ((s8[9437184]{0:T(1024)(128)(4,1)}), s8[4194304]{0:T(1024)(128)(4,1)S(1)}, s32[]{:S(2)}) async-start(s8[9437184]{0:T(1024)(128)(4,1)} %bitcast.57), calls=%async_computation.4 | async-start | bytes 8388608 | tf_op jit(solution)/shard_map/while/body/eval_jaxpr/cond
  451.7 13.3 %slice-start.2 = ((s8[9437184]{0:T(1024)(128)(4,1)}), s8[1048576]{0:T(1024)(128)(4,1)S(1)}, s32[]{:S(2)}) async-start(s8[9437184]{0:T(1024)(128)(4,1)} %bitcast.57), calls=%async_computation.5 | async-start | bytes 2097152 | tf_op jit(solution)/shard_map/while/body/eval_jaxpr/cond
  468.4 8.8 %collective-permute-start.1 = (bf16[1,64,1536]{2,1,0:T(8,128)(2,1)S(1)}, bf16[1,64,1536]{2,1,0:T(8,128)(2,1)S(1)}, u32[]{:S(2)}, u32[]{:S(2)}) collective-permute-start(bf16[1,64,1536]{2,1,0:T(8,128)(2,1)S(1)} %get-tuple-element.616), channel_id=1, source_target_pairs={{96,0},{192,96},{288,192},{384,288},{480,384},{576,480},{672,576},... | collective-permute-start | bytes 589832 | tf_op jit(solution)/shard_map/while/body/eval_jaxpr/ppermute | solution.py:10
  477.6 18.9 %slice-start = ((s8[9437184]{0:T(1024)(128)(4,1)}), s8[4194304]{0:T(1024)(128)(4,1)S(1)}, s32[]{:S(2)}) async-start(s8[9437184]{0:T(1024)(128)(4,1)} %bitcast.57), calls=%async_computation.3 | async-start | bytes 8388608 | tf_op jit(solution)/shard_map/while/body/eval_jaxpr/cond
  483.2 13.3 %slice-start.1 = ((s8[9437184]{0:T(1024)(128)(4,1)}), s8[4194304]{0:T(1024)(128)(4,1)S(1)}, s32[]{:S(2)}) async-start(s8[9437184]{0:T(1024)(128)(4,1)} %bitcast.57), calls=%async_computation.4 | async-start | bytes 8388608 | tf_op jit(solution)/shard_map/while/body/eval_jaxpr/cond
  483.3 13.3 %slice-start.2 = ((s8[9437184]{0:T(1024)(128)(4,1)}), s8[1048576]{0:T(1024)(128)(4,1)S(1)}, s32[]{:S(2)}) async-start(s8[9437184]{0:T(1024)(128)(4,1)} %bitcast.57), calls=%async_computation.5 | async-start | bytes 2097152 | tf_op jit(solution)/shard_map/while/body/eval_jaxpr/cond
  499.9 7.6 collective-permute-start.1
  507.5 27.8 %collective-permute-start.1 = (bf16[1,64,1536]{2,1,0:T(8,128)(2,1)S(1)}, bf16[1,64,1536]{2,1,0:T(8,128)(2,1)S(1)}, u32[]{:S(2)}, u32[]{:S(2)}) collective-permute-start(bf16[1,64,1536]{2,1,0:T(8,128)(2,1)S(1)} %get-tuple-element.616), channel_id=1, source_target_pairs={{96,0},{192,96},{288,192},{384,288},{480,384},{576,480},{672,576},... | collective-permute-start | bytes 589832 | tf_op jit(solution)/shard_map/while/body/eval_jaxpr/ppermute | solution.py:10
Sparse Core Ops, SparseCore 0:
  11.1 131.0 all-gather.2
  535.5 255.2 reduce-scatter.1
where the time goes:
time: 798 us
  waiting for transfers between devices  627 us (79%)
  starting transfers between devices  87.3 us (11%)
  matrix products  55.6 us (7%)
  between operations  14.1 us (2%)
  local copies, waits for them, and re-layouts  9.6 us (1%)
    reduce_scatter x1, waiting for transfers between devices, shards(): lax.psum_scatter(total.reshape(2, width, width), 'shard', scatter_dimensi...  255 us
    ppermute x18, waiting for transfers between devices, from_behind(): return lax.ppermute(block, axis, route)  238 us
    all_gather x1, waiting for transfers between devices, shards(): gathered = lax.all_gather(weights[0], 'shard', axis=1, tiled=True)  132 us
    ppermute x18, starting transfers between devices, from_behind(): return lax.ppermute(block, axis, route)  87.2 us
    dot_general x2, matrix products, run(): lax.dot_general(both, d_pre, (((0,), (0,)), ((), ())), preferred_element_...  26.5 us
  transfers between devices with their start and end apart: 20, of which 20 were waited for; matrix products, arithmetic and copies ran while one was open for 0% of the time, Pallas kernels for 0%

commit v1 on v0

v1 whole, which is shorter than its diff:
```python
import jax
import jax.numpy as jnp
from jax import lax
from jax.experimental import pallas as pl
from jax.experimental.pallas import tpu as pltpu
from jax.sharding import Mesh, PartitionSpec as P

SECTIONS, DEPTH, ACROSS, CORES = 8, 12, 4, 2
PARTS = DEPTH * ACROSS * CORES
OWN = 16
BLOCK = 256
SHARD = ("z", "x", "core")
GROUP = ("x", "core")


def shifted(values, hours, limit_low):
    length = values.shape[0]
    row = lax.broadcasted_iota(jnp.int32, values.shape, 0)
    if limit_low:
        return jnp.where(row >= hours, pltpu.roll(values, hours, 0), 0.0)
    return jnp.where(row < length - hours, pltpu.roll(values, length - hours, 0), 0.0)


def norm_of(x_full):
    inverse = lax.rsqrt(jnp.mean(x_full * x_full, axis=-1, keepdims=True) + 1e-06)
    return inverse, x_full * inverse


def forward_body(meta, x_ref, w_ref, keep_x, keep_z, keep_a, x_out, xs, zs, acts, now, late):
    step = pl.program_id(0)
    del keep_x, keep_z, keep_a

    @pl.when(step == 0)
    def _():
        x_full = x_ref[...].astype(jnp.float32)
        _, normed = norm_of(x_full)
        rounded = normed.astype(jnp.bfloat16)
        now[...] = rounded
        late[...] = shifted(rounded.astype(jnp.float32), meta[1], True).astype(jnp.bfloat16)
        xs[0] = x_ref[...]
        acts[0] = rounded

    rows = now.shape[1]
    pre = jnp.dot(now[...], w_ref[:, 0].reshape(rows, BLOCK), preferred_element_type=jnp.float32)
    pre += jnp.dot(late[...], w_ref[:, 1].reshape(rows, BLOCK), preferred_element_type=jnp.float32)
    zs[0] = pre
    own = x_ref[:, pl.ds(pl.multiple_of(step * BLOCK, BLOCK), BLOCK)].astype(jnp.float32)
    x_out[...] = (own + pre * jax.nn.sigmoid(pre)).astype(jnp.bfloat16)


def layer_forward(meta, x_in, w_all, xs, zs, acts):
    length, width = x_in.shape
    any_spec = pl.BlockSpec(memory_space=pl.ANY)
    return pl.pallas_call(
        forward_body,
        out_shape=(
            jax.ShapeDtypeStruct(x_in.shape, x_in.dtype),
            jax.ShapeDtypeStruct(xs.shape, xs.dtype),
            jax.ShapeDtypeStruct(zs.shape, zs.dtype),
            jax.ShapeDtypeStruct(acts.shape, acts.dtype),
        ),
        grid_spec=pltpu.PrefetchScalarGridSpec(
            num_scalar_prefetch=1,
            grid=(width // BLOCK,),
            in_specs=[
                pl.BlockSpec((length, width), lambda j, meta: (0, 0)),
                pl.BlockSpec((PARTS, 2, OWN, BLOCK), lambda j, meta: (0, 0, 0, j)),
                any_spec,
                any_spec,
                any_spec,
            ],
            out_specs=[
                pl.BlockSpec((length, BLOCK), lambda j, meta: (0, j)),
                pl.BlockSpec((1, length, width), lambda j, meta: (meta[0], 0, 0)),
                pl.BlockSpec((1, length, BLOCK), lambda j, meta: (meta[0], 0, j)),
                pl.BlockSpec((1, length, width), lambda j, meta: (meta[0], 0, 0)),
            ],
            scratch_shapes=[
                pltpu.VMEM((length, width), jnp.bfloat16),
                pltpu.VMEM((length, width), jnp.bfloat16),
            ],
        ),
        input_output_aliases={3: 1, 4: 2, 5: 3},
        compiler_params=pltpu.CompilerParams(vmem_limit_bytes=32 * 1024 * 1024),
        name="layer_forward",
    )(meta, x_in, w_all, xs, zs, acts)


def backward_body(meta, g_ref, x_ref, z_ref, w_ref, keep_d, g_out, dzs, now, early, da):
    step = pl.program_id(0)
    last = pl.num_programs(0) - 1
    del keep_d

    @pl.when(step == 0)
    def _():
        pre = z_ref[0]
        sigma = jax.nn.sigmoid(pre)
        d_pre = g_ref[...].astype(jnp.float32) * sigma * (1.0 + pre * (1.0 - sigma))
        d_pre = d_pre.astype(jnp.bfloat16)
        now[...] = d_pre
        early[...] = shifted(d_pre.astype(jnp.float32), meta[1], False).astype(jnp.bfloat16)
        dzs[0] = d_pre

    width = now.shape[1]
    dims = (((1,), (1,)), ((), ()))
    part = lax.dot_general(now[...], w_ref[:, 0].reshape(BLOCK, width), dims, preferred_element_type=jnp.float32)
    part += lax.dot_general(early[...], w_ref[:, 1].reshape(BLOCK, width), dims, preferred_element_type=jnp.float32)
    da[:, pl.ds(pl.multiple_of(step * BLOCK, BLOCK), BLOCK)] = part

    @pl.when(step == last)
    def _():
        inverse, normed = norm_of(x_ref[0].astype(jnp.float32))
        d_norm = da[...]
        mean = jnp.mean(d_norm * normed, axis=-1, keepdims=True)
        d_x = g_ref[...].astype(jnp.float32) + inverse * (d_norm - normed * mean)
        g_out[...] = d_x.astype(jnp.bfloat16)


def layer_backward(meta, g_in, xs, zs, w_all, dzs):
    length, width = g_in.shape
    return pl.pallas_call(
        backward_body,
        out_shape=(
            jax.ShapeDtypeStruct(g_in.shape, g_in.dtype),
            jax.ShapeDtypeStruct(dzs.shape, dzs.dtype),
        ),
        grid_spec=pltpu.PrefetchScalarGridSpec(
            num_scalar_prefetch=1,
            grid=(width // BLOCK,),
            in_specs=[
                pl.BlockSpec((length, width), lambda j, meta: (0, 0)),
                pl.BlockSpec((1, length, width), lambda j, meta: (meta[0], 0, 0)),
                pl.BlockSpec((1, length, width), lambda j, meta: (meta[0], 0, 0)),
                pl.BlockSpec((BLOCK // OWN, 2, OWN, width), lambda j, meta: (j, 0, 0, 0)),
                pl.BlockSpec(memory_space=pl.ANY),
            ],
            out_specs=[
                pl.BlockSpec((length, width), lambda j, meta: (0, 0)),
                pl.BlockSpec((1, length, width), lambda j, meta: (meta[0], 0, 0)),
            ],
            scratch_shapes=[
                pltpu.VMEM((length, width), jnp.bfloat16),
                pltpu.VMEM((length, width), jnp.bfloat16),
                pltpu.VMEM((length, width), jnp.float32),
            ],
        ),
        input_output_aliases={5: 1},
        compiler_params=pltpu.CompilerParams(vmem_limit_bytes=32 * 1024 * 1024),
        name="layer_backward",
    )(meta, g_in, xs, zs, w_all, dzs)


def advanced(values, hours):
    length = values.shape[-2]
    padded = jnp.concatenate([values, jnp.zeros_like(values)], axis=-2)
    return lax.dynamic_slice_in_dim(padded, hours, length, axis=values.ndim - 2)


def shards(features, index, table, exponent, weights, cotangent):
    here = lax.axis_index("section")
    micro, _, length, width = features.shape
    hours = jnp.left_shift(jnp.int32(1), exponent[0])
    onehot = (index[:, :, None] == jnp.arange(table.shape[0], dtype=jnp.int32)).astype(jnp.bfloat16)
    bias = jnp.einsum("mwb,bc->mwc", onehot, table, preferred_element_type=jnp.float32)
    inputs = (features.astype(jnp.float32) + bias[:, :, None, :]).astype(jnp.bfloat16)[:, 0]
    upstream = cotangent[:, 0]
    w_all = lax.all_gather(weights[0], SHARD, axis=0, tiled=False)

    ticks = SECTIONS + micro - 1
    slots = (micro + 1, length, width)
    xs = jnp.zeros(slots, jnp.bfloat16)
    acts = jnp.zeros(slots, jnp.bfloat16)
    zs = jnp.zeros(slots, jnp.float32)
    dzs = jnp.zeros(slots, jnp.bfloat16)

    def meta_of(order):
        inside = jnp.logical_and(order >= 0, order < micro)
        return jnp.stack([jnp.where(inside, order, micro), hours]).astype(jnp.int32)

    upward = [(i, i + 1) for i in range(SECTIONS - 1)]
    downward = [(i + 1, i) for i in range(SECTIONS - 1)]

    block = inputs[0]
    for tick in range(ticks):
        if 0 < tick < micro:
            block = jnp.where(here == 0, inputs[tick], block)
        block, xs, zs, acts = layer_forward(meta_of(tick - here), block, w_all, xs, zs, acts)
        if tick < ticks - 1:
            block = lax.ppermute(block, "section", upward)

    every = lax.all_gather(acts[:micro], GROUP, axis=0, tiled=False)

    grad = upstream[0]
    for tick in range(ticks):
        if 0 < tick < micro:
            grad = jnp.where(here == SECTIONS - 1, upstream[tick], grad)
        grad, dzs = layer_backward(meta_of(tick - (SECTIONS - 1 - here)), grad, xs, zs, w_all, dzs)
        if tick < ticks - 1:
            grad = lax.ppermute(grad, "section", downward)

    members = ACROSS * CORES
    piece = width // members
    rows = micro * length
    mine = dzs[:micro].reshape(rows, members, piece).transpose(1, 0, 2)
    theirs = lax.all_to_all(mine, GROUP, 0, 0, tiled=True)
    theirs = theirs.reshape(members * micro, length, piece)
    sides = jnp.concatenate([theirs, advanced(theirs, hours)], axis=-1).reshape(members * rows, 2 * piece)
    partial = lax.dot_general(
        every.reshape(members * rows, width), sides, (((0,), (0,)), ((), ())), preferred_element_type=jnp.float32
    ).astype(jnp.bfloat16)
    spread = lax.all_to_all(partial.reshape(DEPTH, members * OWN, 2 * piece), "z", 0, 0, tiled=True)
    total = jnp.sum(spread.astype(jnp.float32), axis=0)
    back = lax.all_to_all(total.reshape(members, OWN, 2 * piece), GROUP, 0, 0, tiled=True)
    owned = back.reshape(members, OWN, 2, piece).transpose(2, 1, 0, 3).reshape(2, OWN, width)
    return owned[None]


def solution(mesh):
    fine = Mesh(mesh.devices.reshape(SECTIONS, DEPTH, ACROSS, CORES), ("section", "z", "x", "core"))
    placed = (
        P(None, SHARD, None, None),
        P(None, SHARD),
        P(),
        P("section"),
        P("section", None, SHARD, None),
        P(None, SHARD, None, None),
    )
    return jax.shard_map(
        shards, mesh=fine, in_specs=placed, out_specs=P("section", None, SHARD, None), check_vma=False
    )
```

time: 798 us -> 523 us (0.66)
  the two profiles are of different devices: /device:TPU:8 before, /device:TPU:24 now
where the time goes in v1:
time: 523 us; the launch traced here: 522 us
  waiting for transfers between devices  224 us (43%)
  Pallas kernels  80.4 us (15%)
  local copies, waits for them, and re-layouts  70.9 us (14%)
  starting transfers between devices  63.2 us (12%)
  blocking collectives  61.1 us (12%)
  between operations  14.7 us (3%)
    all_gather x1, waiting for transfers between devices, shards(): w_all = lax.all_gather(weights[0], SHARD, axis=0, tiled=False)  132 us
    unnamed x40, local copies, waits for them, and re-layouts  66.5 us
    ppermute x8, waiting for transfers between devices, shards(): grad = lax.ppermute(grad, 'section', downward)  56.1 us
    all_to_all x1, blocking collectives, shards(): lax.all_to_all(partial.reshape(DEPTH, members * OWN, 2 * piece), 'z', 0,...  51.9 us
    ppermute x8, starting transfers between devices, shards(): block = lax.ppermute(block, 'section', upward)  43.8 us
    pallas_call x9, Pallas kernels, layer_backward(): pl.pallas_call(backward_body, out_shape=(jax.ShapeDtypeStruct(g_in.shape,...  43 us
    pallas_call x9, Pallas kernels, layer_forward(): pl.pallas_call(forward_body, out_shape=(jax.ShapeDtypeStruct(x_in.shape,...  37.3 us
    ppermute x8, waiting for transfers between devices, shards(): block = lax.ppermute(block, 'section', upward)  26.6 us
  transfers between devices with their start and end apart: 19, of which 18 were waited for; matrix products, arithmetic and copies ran while one was open for 1% of the time, Pallas kernels for 8%

profile of v1, /device:TPU:24, one launch (start us, length us, event | category | flops | bytes accessed | tf_op | source)
XLA Modules:
  0.0 522.0 jit_solution(584877167290557284)
XLA Ops:
  10.0 131.9 %all-gather.4.cloned.1.call-done.w_ref = bf16[96,2,16,1536]{3,2,1,0:T(8,128)(2,1)} async-done(((bf16[1,2,16,1536]{3,2,1,0:T(8,128)(2,1)}), bf16[96,2,16,1536]{3,2,1,0:T(8,128)(2,1)}) %all-gather.4.cloned.1.call-update) | async-done | bytes 9437200 | tf_op jit(solution)/shard_map/all_gather | solution.py:167
  142.1 3.7 copy-done.1
  145.8 4.1 layer_forward.9
  149.9 4.6 collective-permute-start
  154.6 4.5 collective-permute-done
  159.1 3.7 copy-done.2
  162.8 4.1 layer_forward.10
  166.9 5.6 %collective-permute-start.1 = (bf16[64,1536]{1,0:T(8,128)(2,1)S(1)}, bf16[64,1536]{1,0:T(8,128)(2,1)S(1)}, u32[]{:S(2)}, u32[]{:S(2)}) collective-permute-start(bf16[64,1536]{1,0:T(8,128)(2,1)S(1)} %get-tuple-element.61), channel_id=1, source_target_pairs={{0,96},{96,192},{192,288},{288,384},{384,480},{480,576},{576,672},... | collective-permute-start | bytes 589832 | tf_op jit(solution)/shard_map/ppermute | solution.py:189
  172.6 3.7 collective-permute-done.1.x_ref
  176.2 3.7 copy-done.3
  179.9 4.1 layer_forward.11
  184.0 5.6 %collective-permute-start.2 = (bf16[64,1536]{1,0:T(8,128)(2,1)S(1)}, bf16[64,1536]{1,0:T(8,128)(2,1)S(1)}, u32[]{:S(2)}, u32[]{:S(2)}) collective-permute-start(bf16[64,1536]{1,0:T(8,128)(2,1)S(1)} %get-tuple-element.65), channel_id=1, source_target_pairs={{0,96},{96,192},{192,288},{288,384},{384,480},{480,576},{576,672},... | collective-permute-start | bytes 589832 | tf_op jit(solution)/shard_map/ppermute | solution.py:189
  192.8 3.7 copy-done.4
  196.4 4.1 layer_forward.12
  200.5 5.6 %collective-permute-start.3 = (bf16[64,1536]{1,0:T(8,128)(2,1)S(1)}, bf16[64,1536]{1,0:T(8,128)(2,1)S(1)}, u32[]{:S(2)}, u32[]{:S(2)}) collective-permute-start(bf16[64,1536]{1,0:T(8,128)(2,1)S(1)} %get-tuple-element.69), channel_id=1, source_target_pairs={{0,96},{96,192},{192,288},{288,384},{384,480},{480,576},{576,672},... | collective-permute-start | bytes 589832 | tf_op jit(solution)/shard_map/ppermute | solution.py:189
  206.2 3.1 collective-permute-done.3.x_ref
  209.3 3.7 copy-done.5
  213.0 4.1 layer_forward.13
  217.1 5.6 %collective-permute-start.4 = (bf16[64,1536]{1,0:T(8,128)(2,1)S(1)}, bf16[64,1536]{1,0:T(8,128)(2,1)S(1)}, u32[]{:S(2)}, u32[]{:S(2)}) collective-permute-start(bf16[64,1536]{1,0:T(8,128)(2,1)S(1)} %get-tuple-element.73), channel_id=1, source_target_pairs={{0,96},{96,192},{192,288},{288,384},{384,480},{480,576},{576,672},... | collective-permute-start | bytes 589832 | tf_op jit(solution)/shard_map/ppermute | solution.py:189
  222.8 3.1 collective-permute-done.4.x_ref
  225.8 3.7 copy-done.6
  229.5 4.1 layer_forward.14
  233.6 5.6 %collective-permute-start.5 = (bf16[64,1536]{1,0:T(8,128)(2,1)S(1)}, bf16[64,1536]{1,0:T(8,128)(2,1)S(1)}, u32[]{:S(2)}, u32[]{:S(2)}) collective-permute-start(bf16[64,1536]{1,0:T(8,128)(2,1)S(1)} %get-tuple-element.77), channel_id=1, source_target_pairs={{0,96},{96,192},{192,288},{288,384},{384,480},{480,576},{576,672},... | collective-permute-start | bytes 589832 | tf_op jit(solution)/shard_map/ppermute | solution.py:189
  242.4 3.7 copy-done.7
  246.1 4.1 layer_forward.15
  250.1 5.6 %collective-permute-start.6 = (bf16[64,1536]{1,0:T(8,128)(2,1)S(1)}, bf16[64,1536]{1,0:T(8,128)(2,1)S(1)}, u32[]{:S(2)}, u32[]{:S(2)}) collective-permute-start(bf16[64,1536]{1,0:T(8,128)(2,1)S(1)} %get-tuple-element.81), channel_id=1, source_target_pairs={{0,96},{96,192},{192,288},{288,384},{384,480},{480,576},{576,672},... | collective-permute-start | bytes 589832 | tf_op jit(solution)/shard_map/ppermute | solution.py:189
  255.8 3.1 collective-permute-done.6.x_ref
  258.9 3.7 copy-done.8
  262.6 4.1 layer_forward.16
  266.7 5.6 %collective-permute-start.7 = (bf16[64,1536]{1,0:T(8,128)(2,1)S(1)}, bf16[64,1536]{1,0:T(8,128)(2,1)S(1)}, u32[]{:S(2)}, u32[]{:S(2)}) collective-permute-start(bf16[64,1536]{1,0:T(8,128)(2,1)S(1)} %get-tuple-element.85), channel_id=1, source_target_pairs={{0,96},{96,192},{192,288},{288,384},{384,480},{480,576},{576,672},... | collective-permute-start | bytes 589832 | tf_op jit(solution)/shard_map/ppermute | solution.py:189
  272.4 3.1 collective-permute-done.7.x_ref
  275.4 3.7 copy-done.9
  279.1 4.8 layer_forward.17
  285.1 3.7 copy-done.10
  288.8 4.7 layer_backward.9
  295.5 7.2 %collective-permute-done.8 = bf16[64,1536]{1,0:T(8,128)(2,1)S(1)} collective-permute-done((bf16[64,1536]{1,0:T(8,128)(2,1)S(1)}, bf16[64,1536]{1,0:T(8,128)(2,1)S(1)}, u32[]{:S(2)}, u32[]{:S(2)}) %collective-permute-start.8) | collective-permute-done | bytes 196640 | tf_op jit(solution)/shard_map/ppermute | solution.py:199
  302.8 3.7 copy-done.11
  306.5 4.7 layer_backward.10
  313.2 6.8 %collective-permute-done.9.g_ref = bf16[64,1536]{1,0:T(8,128)(2,1)S(1)} collective-permute-done((bf16[64,1536]{1,0:T(8,128)(2,1)S(1)}, bf16[64,1536]{1,0:T(8,128)(2,1)S(1)}, u32[]{:S(2)}, u32[]{:S(2)}) %collective-permute-start.9) | collective-permute-done | bytes 196640 | tf_op jit(solution)/shard_map/ppermute | solution.py:199
  320.0 3.7 copy-done.12
  323.7 4.7 layer_backward.11
  330.4 6.8 %collective-permute-done.10.g_ref = bf16[64,1536]{1,0:T(8,128)(2,1)S(1)} collective-permute-done((bf16[64,1536]{1,0:T(8,128)(2,1)S(1)}, bf16[64,1536]{1,0:T(8,128)(2,1)S(1)}, u32[]{:S(2)}, u32[]{:S(2)}) %collective-permute-start.10) | collective-permute-done | bytes 196640 | tf_op jit(solution)/shard_map/ppermute | solution.py:199
  337.1 3.7 copy-done.13
  340.8 4.7 layer_backward.12
  347.6 6.8 %collective-permute-done.11.g_ref = bf16[64,1536]{1,0:T(8,128)(2,1)S(1)} collective-permute-done((bf16[64,1536]{1,0:T(8,128)(2,1)S(1)}, bf16[64,1536]{1,0:T(8,128)(2,1)S(1)}, u32[]{:S(2)}, u32[]{:S(2)}) %collective-permute-start.11) | collective-permute-done | bytes 196640 | tf_op jit(solution)/shard_map/ppermute | solution.py:199
  354.3 3.7 copy-done.14
  358.0 4.7 layer_backward.13
  364.7 6.8 %collective-permute-done.12.g_ref = bf16[64,1536]{1,0:T(8,128)(2,1)S(1)} collective-permute-done((bf16[64,1536]{1,0:T(8,128)(2,1)S(1)}, bf16[64,1536]{1,0:T(8,128)(2,1)S(1)}, u32[]{:S(2)}, u32[]{:S(2)}) %collective-permute-start.12) | collective-permute-done | bytes 196640 | tf_op jit(solution)/shard_map/ppermute | solution.py:199
  371.5 3.7 copy-done.15
  375.2 4.7 layer_backward.14
  382.1 6.9 %collective-permute-done.13.g_ref = bf16[64,1536]{1,0:T(8,128)(2,1)S(1)} collective-permute-done((bf16[64,1536]{1,0:T(8,128)(2,1)S(1)}, bf16[64,1536]{1,0:T(8,128)(2,1)S(1)}, u32[]{:S(2)}, u32[]{:S(2)}) %collective-permute-start.13) | collective-permute-done | bytes 196640 | tf_op jit(solution)/shard_map/ppermute | solution.py:199
  389.0 3.7 copy-done.16
  392.6 4.7 layer_backward.15
  399.4 8.3 %collective-permute-done.14.g_ref = bf16[64,1536]{1,0:T(8,128)(2,1)S(1)} collective-permute-done((bf16[64,1536]{1,0:T(8,128)(2,1)S(1)}, bf16[64,1536]{1,0:T(8,128)(2,1)S(1)}, u32[]{:S(2)}, u32[]{:S(2)}) %collective-permute-start.14) | collective-permute-done | bytes 196640 | tf_op jit(solution)/shard_map/ppermute | solution.py:199
  407.6 3.7 copy-done.17
  411.3 4.7 layer_backward.16
  418.0 6.8 %collective-permute-done.15.g_ref = bf16[64,1536]{1,0:T(8,128)(2,1)S(1)} collective-permute-done((bf16[64,1536]{1,0:T(8,128)(2,1)S(1)}, bf16[64,1536]{1,0:T(8,128)(2,1)S(1)}, u32[]{:S(2)}, u32[]{:S(2)}) %collective-permute-start.15) | collective-permute-done | bytes 196640 | tf_op jit(solution)/shard_map/ppermute | solution.py:199
  424.8 3.7 copy-done.18
  428.5 5.4 %layer_backward.17 = (bf16[64,1536]{1,0:T(8,128)(2,1)}, bf16[3,64,1536]{2,1,0:T(8,128)(2,1)S(1)}) custom-call(s32[2]{0:T(128)S(1)} %pad_add_fusion.9.meta, bf16[64,1536]{1,0:T(8,128)(2,1)S(1)} %collective-permute-done.15.g_ref, bf16[3,64,1536]{2,1,0:T(8,128)(2,1)S(1)} %get-tuple-element.90.x_ref, ...), custom_call_target="tpu_custom_call", output_to_operand_aliasing={{1}: (5, {})} | custom-call | tf_op jit(solution)/shard_map/layer_backward/pallas_call | solution.py:121
  435.4 3.8 all-to-all-start
  439.3 8.9 %all-to-all-done = bf16[8,128,192]{1,2,0:T(8,128)(2,1)S(1)} async-done(((bf16[8,128,192]{1,2,0:T(8,128)(2,1)}), bf16[8,128,192]{1,2,0:T(8,128)(2,1)S(1)}, u32[]{:S(2)}, u32[]{:S(2)}) %all-to-all-start) | async-done | bytes 393248 | tf_op jit(solution)/shard_map/all_to_all | solution.py:205
  448.9 3.7 convolution_convert_fusion
  452.7 51.9 %all_to_all.15 = bf16[12,128,384]{2,1,0:T(8,128)(2,1)S(1)} all-to-all(bf16[12,128,384]{2,1,0:T(8,128)(2,1)S(1)} %bitcast.49), channel_id=1, replica_groups=mesh['section'=8,'z'=12,'x'=4,'core'=2] {'z'}, dimensions={0} | all-to-all | bytes 2359296 | tf_op jit(solution)/shard_map/all_to_all | solution.py:211
  504.7 9.2 %all_to_all.16 = f32[8,16,384]{2,1,0:T(8,128)S(1)} all-to-all(f32[8,16,384]{2,1,0:T(8,128)S(1)} %bitcast.51), channel_id=1, replica_groups=mesh['section'=8,'z'=12,'x'=4,'core'=2] {'x','core'}, dimensions={0} | all-to-all | bytes 393216 | tf_op jit(solution)/shard_map/all_to_all | solution.py:213
  (77 shorter events, 30.7 us)
Async XLA Ops:
  6.5 1.5 copy-start
  6.5 135.4 %all-gather.4.cloned.1.call-start = ((), (), s32[]{:S(2)}) async-start(), calls=%async_computation.3 | async-start | bytes 9535488 | tf_op jit(solution)/shard_map/all_gather | solution.py:167
  7.3 441.7 %all-gather.6.cloned.1.call-start = ((), (), s32[]{:S(2)}) async-start(), calls=%async_computation.4 | async-start | bytes 3538944 | tf_op jit(solution)/shard_map/all_gather | solution.py:191
  142.1 3.7 copy-start.1
  149.9 9.2 %collective-permute-start = (bf16[64,1536]{1,0:T(8,128)(2,1)S(1)}, bf16[64,1536]{1,0:T(8,128)(2,1)S(1)}, u32[]{:S(2)}, u32[]{:S(2)}) collective-permute-start(bf16[64,1536]{1,0:T(8,128)(2,1)S(1)} %get-tuple-element.57), channel_id=1, source_target_pairs={{0,96},{96,192},{192,288},{288,384},{384,480},{480,576},{576,672},... | collective-permute-start | bytes 589832 | tf_op jit(solution)/shard_map/ppermute | solution.py:189
  159.1 3.7 copy-start.2
  166.9 9.4 %collective-permute-start.1 = (bf16[64,1536]{1,0:T(8,128)(2,1)S(1)}, bf16[64,1536]{1,0:T(8,128)(2,1)S(1)}, u32[]{:S(2)}, u32[]{:S(2)}) collective-permute-start(bf16[64,1536]{1,0:T(8,128)(2,1)S(1)} %get-tuple-element.61), channel_id=1, source_target_pairs={{0,96},{96,192},{192,288},{288,384},{384,480},{480,576},{576,672},... | collective-permute-start | bytes 589832 | tf_op jit(solution)/shard_map/ppermute | solution.py:189
  176.2 3.7 copy-start.3
  184.0 8.8 %collective-permute-start.2 = (bf16[64,1536]{1,0:T(8,128)(2,1)S(1)}, bf16[64,1536]{1,0:T(8,128)(2,1)S(1)}, u32[]{:S(2)}, u32[]{:S(2)}) collective-permute-start(bf16[64,1536]{1,0:T(8,128)(2,1)S(1)} %get-tuple-element.65), channel_id=1, source_target_pairs={{0,96},{96,192},{192,288},{288,384},{384,480},{480,576},{576,672},... | collective-permute-start | bytes 589832 | tf_op jit(solution)/shard_map/ppermute | solution.py:189
  192.8 3.7 copy-start.4
  200.5 8.8 %collective-permute-start.3 = (bf16[64,1536]{1,0:T(8,128)(2,1)S(1)}, bf16[64,1536]{1,0:T(8,128)(2,1)S(1)}, u32[]{:S(2)}, u32[]{:S(2)}) collective-permute-start(bf16[64,1536]{1,0:T(8,128)(2,1)S(1)} %get-tuple-element.69), channel_id=1, source_target_pairs={{0,96},{96,192},{192,288},{288,384},{384,480},{480,576},{576,672},... | collective-permute-start | bytes 589832 | tf_op jit(solution)/shard_map/ppermute | solution.py:189
  209.3 3.7 copy-start.5
  217.1 8.8 %collective-permute-start.4 = (bf16[64,1536]{1,0:T(8,128)(2,1)S(1)}, bf16[64,1536]{1,0:T(8,128)(2,1)S(1)}, u32[]{:S(2)}, u32[]{:S(2)}) collective-permute-start(bf16[64,1536]{1,0:T(8,128)(2,1)S(1)} %get-tuple-element.73), channel_id=1, source_target_pairs={{0,96},{96,192},{192,288},{288,384},{384,480},{480,576},{576,672},... | collective-permute-start | bytes 589832 | tf_op jit(solution)/shard_map/ppermute | solution.py:189
  225.8 3.7 copy-start.6
  233.6 8.8 %collective-permute-start.5 = (bf16[64,1536]{1,0:T(8,128)(2,1)S(1)}, bf16[64,1536]{1,0:T(8,128)(2,1)S(1)}, u32[]{:S(2)}, u32[]{:S(2)}) collective-permute-start(bf16[64,1536]{1,0:T(8,128)(2,1)S(1)} %get-tuple-element.77), channel_id=1, source_target_pairs={{0,96},{96,192},{192,288},{288,384},{384,480},{480,576},{576,672},... | collective-permute-start | bytes 589832 | tf_op jit(solution)/shard_map/ppermute | solution.py:189
  242.4 3.7 copy-start.7
  250.1 8.8 %collective-permute-start.6 = (bf16[64,1536]{1,0:T(8,128)(2,1)S(1)}, bf16[64,1536]{1,0:T(8,128)(2,1)S(1)}, u32[]{:S(2)}, u32[]{:S(2)}) collective-permute-start(bf16[64,1536]{1,0:T(8,128)(2,1)S(1)} %get-tuple-element.81), channel_id=1, source_target_pairs={{0,96},{96,192},{192,288},{288,384},{384,480},{480,576},{576,672},... | collective-permute-start | bytes 589832 | tf_op jit(solution)/shard_map/ppermute | solution.py:189
  258.9 3.7 copy-start.8
  266.7 8.8 %collective-permute-start.7 = (bf16[64,1536]{1,0:T(8,128)(2,1)S(1)}, bf16[64,1536]{1,0:T(8,128)(2,1)S(1)}, u32[]{:S(2)}, u32[]{:S(2)}) collective-permute-start(bf16[64,1536]{1,0:T(8,128)(2,1)S(1)} %get-tuple-element.85), channel_id=1, source_target_pairs={{0,96},{96,192},{192,288},{288,384},{384,480},{480,576},{576,672},... | collective-permute-start | bytes 589832 | tf_op jit(solution)/shard_map/ppermute | solution.py:189
  275.4 3.7 copy-start.9
  283.9 1.1 copy-start.19
  285.1 3.7 copy-start.10
  293.5 9.2 %collective-permute-start.8 = (bf16[64,1536]{1,0:T(8,128)(2,1)S(1)}, bf16[64,1536]{1,0:T(8,128)(2,1)S(1)}, u32[]{:S(2)}, u32[]{:S(2)}) collective-permute-start(bf16[64,1536]{1,0:T(8,128)(2,1)S(1)} %get-tuple-element.92), channel_id=1, source_target_pairs={{96,0},{192,96},{288,192},{384,288},{480,384},{576,480},{672,576},... | collective-permute-start | bytes 589832 | tf_op jit(solution)/shard_map/ppermute | solution.py:199
  302.8 3.7 copy-start.11
  311.2 8.8 %collective-permute-start.9 = (bf16[64,1536]{1,0:T(8,128)(2,1)S(1)}, bf16[64,1536]{1,0:T(8,128)(2,1)S(1)}, u32[]{:S(2)}, u32[]{:S(2)}) collective-permute-start(bf16[64,1536]{1,0:T(8,128)(2,1)S(1)} %get-tuple-element.94), channel_id=1, source_target_pairs={{96,0},{192,96},{288,192},{384,288},{480,384},{576,480},{672,576},... | collective-permute-start | bytes 589832 | tf_op jit(solution)/shard_map/ppermute | solution.py:199
  320.0 3.7 copy-start.12
  328.4 8.8 %collective-permute-start.10 = (bf16[64,1536]{1,0:T(8,128)(2,1)S(1)}, bf16[64,1536]{1,0:T(8,128)(2,1)S(1)}, u32[]{:S(2)}, u32[]{:S(2)}) collective-permute-start(bf16[64,1536]{1,0:T(8,128)(2,1)S(1)} %get-tuple-element.96), channel_id=1, source_target_pairs={{96,0},{192,96},{288,192},{384,288},{480,384},{576,480},{672,576},... | collective-permute-start | bytes 589832 | tf_op jit(solution)/shard_map/ppermute | solution.py:199
  337.1 3.7 copy-start.13
  345.5 8.8 %collective-permute-start.11 = (bf16[64,1536]{1,0:T(8,128)(2,1)S(1)}, bf16[64,1536]{1,0:T(8,128)(2,1)S(1)}, u32[]{:S(2)}, u32[]{:S(2)}) collective-permute-start(bf16[64,1536]{1,0:T(8,128)(2,1)S(1)} %get-tuple-element.98), channel_id=1, source_target_pairs={{96,0},{192,96},{288,192},{384,288},{480,384},{576,480},{672,576},... | collective-permute-start | bytes 589832 | tf_op jit(solution)/shard_map/ppermute | solution.py:199
  354.3 3.7 copy-start.14
  362.7 8.8 %collective-permute-start.12 = (bf16[64,1536]{1,0:T(8,128)(2,1)S(1)}, bf16[64,1536]{1,0:T(8,128)(2,1)S(1)}, u32[]{:S(2)}, u32[]{:S(2)}) collective-permute-start(bf16[64,1536]{1,0:T(8,128)(2,1)S(1)} %get-tuple-element.100), channel_id=1, source_target_pairs={{96,0},{192,96},{288,192},{384,288},{480,384},{576,480},{672,576},... | collective-permute-start | bytes 589832 | tf_op jit(solution)/shard_map/ppermute | solution.py:199
  371.5 3.7 copy-start.15
  379.9 9.1 %collective-permute-start.13 = (bf16[64,1536]{1,0:T(8,128)(2,1)S(1)}, bf16[64,1536]{1,0:T(8,128)(2,1)S(1)}, u32[]{:S(2)}, u32[]{:S(2)}) collective-permute-start(bf16[64,1536]{1,0:T(8,128)(2,1)S(1)} %get-tuple-element.102), channel_id=1, source_target_pairs={{96,0},{192,96},{288,192},{384,288},{480,384},{576,480},{672,576},... | collective-permute-start | bytes 589832 | tf_op jit(solution)/shard_map/ppermute | solution.py:199
  389.0 3.7 copy-start.16
  397.3 10.3 %collective-permute-start.14 = (bf16[64,1536]{1,0:T(8,128)(2,1)S(1)}, bf16[64,1536]{1,0:T(8,128)(2,1)S(1)}, u32[]{:S(2)}, u32[]{:S(2)}) collective-permute-start(bf16[64,1536]{1,0:T(8,128)(2,1)S(1)} %get-tuple-element.104), channel_id=1, source_target_pairs={{96,0},{192,96},{288,192},{384,288},{480,384},{576,480},{672,576},... | collective-permute-start | bytes 589832 | tf_op jit(solution)/shard_map/ppermute | solution.py:199
  407.6 3.7 copy-start.17
  416.0 8.8 %collective-permute-start.15 = (bf16[64,1536]{1,0:T(8,128)(2,1)S(1)}, bf16[64,1536]{1,0:T(8,128)(2,1)S(1)}, u32[]{:S(2)}, u32[]{:S(2)}) collective-permute-start(bf16[64,1536]{1,0:T(8,128)(2,1)S(1)} %get-tuple-element.106), channel_id=1, source_target_pairs={{96,0},{192,96},{288,192},{384,288},{480,384},{576,480},{672,576},... | collective-permute-start | bytes 589832 | tf_op jit(solution)/shard_map/ppermute | solution.py:199
  424.8 3.7 copy-start.18
  435.4 12.8 %all-to-all-start = ((bf16[8,128,192]{1,2,0:T(8,128)(2,1)}), bf16[8,128,192]{1,2,0:T(8,128)(2,1)S(1)}, u32[]{:S(2)}, u32[]{:S(2)}) async-start(bf16[8,128,192]{1,2,0:T(8,128)(2,1)} %copy.50), calls=%async_computation | async-start | bytes 786432 | tf_op jit(solution)/shard_map/all_to_all | solution.py:205
Sparse Core Ops, SparseCore 0:
  11.0 130.8 all-gather.3
  284.8 32.9 all-gather.5

commit v2 on v1

v2 whole, which is shorter than its diff:
```python
import jax
import jax.numpy as jnp
from jax import lax
from jax.experimental import pallas as pl
from jax.experimental.pallas import tpu as pltpu
from jax.sharding import Mesh, PartitionSpec as P

SECTIONS, HIGH, LOW, ACROSS, CORES = 8, 4, 3, 4, 2
OWN = 16
BLOCK = 256
LIMIT = 20 * 1024 * 1024
SHARD = ("zh", "zl", "x", "core")
DEEP = ("zh", "zl")
ROW = ("x", "core")
WIDE = ("zl", "x", "core")


def shifted(values, hours, limit_low):
    length = values.shape[0]
    row = lax.broadcasted_iota(jnp.int32, values.shape, 0)
    if limit_low:
        return jnp.where(row >= hours, pltpu.roll(values, hours, 0), 0.0)
    return jnp.where(row < length - hours, pltpu.roll(values, length - hours, 0), 0.0)


def norm_of(x_full):
    inverse = lax.rsqrt(jnp.mean(x_full * x_full, axis=-1, keepdims=True) + 1e-06)
    return inverse, x_full * inverse


def settle_body(own_in, other_in, after, own, other, sems):
    del after
    copies = [
        pltpu.make_async_copy(own_in, own, sems.at[0]),
        pltpu.make_async_copy(other_in, other, sems.at[1]),
    ]
    for copy in copies:
        copy.start()
    for copy in copies:
        copy.wait()


def settle(own, other, after):
    size = own.size * own.dtype.itemsize
    return pl.pallas_call(
        settle_body,
        out_shape=(pltpu.VMEM(own.shape, own.dtype), pltpu.VMEM(other.shape, other.dtype)),
        in_specs=[pl.BlockSpec(memory_space=pltpu.HBM)] * 2 + [pl.BlockSpec(memory_space=pl.ANY)],
        out_specs=[pl.BlockSpec(memory_space=pltpu.VMEM)] * 2,
        scratch_shapes=[pltpu.SemaphoreType.DMA((2,))],
        cost_estimate=pl.CostEstimate(flops=0, transcendentals=0, bytes_accessed=4 * size),
        compiler_params=pltpu.CompilerParams(vmem_limit_bytes=LIMIT),
        name="settle",
    )(pltpu.with_memory_space_constraint(own, pltpu.HBM), pltpu.with_memory_space_constraint(other, pltpu.HBM), after)


def ordered(meta, current, moved):
    even = meta[2] == 0
    first = jnp.where(even, current, moved).astype(jnp.bfloat16)
    second = jnp.where(even, moved, current).astype(jnp.bfloat16)
    return first, second


def forward_body(meta, x_ref, own_ref, other_ref, keep_x, keep_z, keep_a, x_out, xs, zs, acts):
    del keep_x, keep_z, keep_a
    slot = meta[0]
    x_full = x_ref[...].astype(jnp.float32)
    _, normed = norm_of(x_full)
    rounded = normed.astype(jnp.bfloat16)
    xs[slot] = x_ref[...]
    acts[slot] = rounded
    current = rounded.astype(jnp.float32)
    first, second = ordered(meta, current, shifted(current, meta[1], True))
    for start in range(0, x_ref.shape[1], BLOCK):
        cols = slice(start, start + BLOCK)
        pre = jnp.dot(first, own_ref[:, cols], preferred_element_type=jnp.float32)
        pre += jnp.dot(second, other_ref[:, cols], preferred_element_type=jnp.float32)
        zs[slot, :, cols] = pre
        x_out[:, cols] = (x_ref[:, cols].astype(jnp.float32) + pre * jax.nn.sigmoid(pre)).astype(jnp.bfloat16)


VMEM = pl.BlockSpec(memory_space=pltpu.VMEM)
SMEM = pl.BlockSpec(memory_space=pltpu.SMEM)


def layer_forward(meta, x_in, own, other, xs, zs, acts):
    return pl.pallas_call(
        forward_body,
        out_shape=tuple(jax.ShapeDtypeStruct(v.shape, v.dtype) for v in (x_in, xs, zs, acts)),
        in_specs=[SMEM] + [VMEM] * 6,
        out_specs=[VMEM] * 4,
        input_output_aliases={4: 1, 5: 2, 6: 3},
        compiler_params=pltpu.CompilerParams(vmem_limit_bytes=LIMIT),
        name="layer_forward",
    )(meta, x_in, own, other, xs, zs, acts)


def backward_body(meta, g_ref, xs, zs, own_ref, other_ref, keep_d, g_out, dzs, da):
    del keep_d
    slot = meta[0]
    pre = zs[slot]
    sigma = jax.nn.sigmoid(pre)
    d_pre = g_ref[...].astype(jnp.float32) * sigma * (1.0 + pre * (1.0 - sigma))
    d_pre = d_pre.astype(jnp.bfloat16)
    dzs[slot] = d_pre
    current = d_pre.astype(jnp.float32)
    first, second = ordered(meta, current, shifted(current, meta[1], False))
    dims = (((1,), (1,)), ((), ()))
    for start in range(0, g_ref.shape[1], BLOCK):
        rows = slice(start, start + BLOCK)
        part = lax.dot_general(first, own_ref[rows, :], dims, preferred_element_type=jnp.float32)
        part += lax.dot_general(second, other_ref[rows, :], dims, preferred_element_type=jnp.float32)
        da[:, rows] = part
    inverse, normed = norm_of(xs[slot].astype(jnp.float32))
    d_norm = da[...]
    mean = jnp.mean(d_norm * normed, axis=-1, keepdims=True)
    g_out[...] = (g_ref[...].astype(jnp.float32) + inverse * (d_norm - normed * mean)).astype(jnp.bfloat16)


def layer_backward(meta, g_in, xs, zs, own, other, dzs):
    return pl.pallas_call(
        backward_body,
        out_shape=tuple(jax.ShapeDtypeStruct(v.shape, v.dtype) for v in (g_in, dzs)),
        in_specs=[SMEM] + [VMEM] * 6,
        out_specs=[VMEM] * 2,
        scratch_shapes=[pltpu.VMEM(g_in.shape, jnp.float32)],
        input_output_aliases={6: 1},
        compiler_params=pltpu.CompilerParams(vmem_limit_bytes=LIMIT),
        name="layer_backward",
    )(meta, g_in, xs, zs, own, other, dzs)


def advanced(values, hours):
    length = values.shape[-2]
    padded = jnp.concatenate([values, jnp.zeros_like(values)], axis=-2)
    return lax.dynamic_slice_in_dim(padded, hours, length, axis=values.ndim - 2)


def shards(features, index, table, exponent, weights, cotangent):
    here = lax.axis_index("section")
    micro, _, length, width = features.shape
    hours = jnp.left_shift(jnp.int32(1), exponent[0])
    onehot = (index[:, :, None] == jnp.arange(table.shape[0], dtype=jnp.int32)).astype(jnp.bfloat16)
    bias = jnp.einsum("mwb,bc->mwc", onehot, table, preferred_element_type=jnp.float32)
    inputs = (features.astype(jnp.float32) + bias[:, :, None, :]).astype(jnp.bfloat16)[:, 0]
    upstream = cotangent[:, 0]
    core = lax.axis_index("core")
    tap = weights[0]
    copies = jnp.broadcast_to(tap[None], (ACROSS,) + tap.shape).reshape(ACROSS * CORES * OWN, width)
    row = lax.all_to_all(copies, ROW, 0, 0, tiled=True)
    own = lax.all_gather(row, DEEP, axis=0, tiled=True)
    other = lax.ppermute(own, "core", [(0, 1), (1, 0)])
    near = settle(own, other, inputs)

    ticks = SECTIONS + micro - 1
    slots = (micro + 1, length, width)
    xs = jnp.zeros(slots, jnp.bfloat16)
    acts = jnp.zeros(slots, jnp.bfloat16)
    zs = jnp.zeros(slots, jnp.float32)
    dzs = jnp.zeros(slots, jnp.bfloat16)

    def meta_of(order):
        inside = jnp.logical_and(order >= 0, order < micro)
        return jnp.stack([jnp.where(inside, order, micro), hours, core]).astype(jnp.int32)

    upward = [(i, i + 1) for i in range(SECTIONS - 1)]
    downward = [(i + 1, i) for i in range(SECTIONS - 1)]

    block = inputs[0]
    for tick in range(ticks):
        if 0 < tick < micro:
            block = jnp.where(here == 0, inputs[tick], block)
        block, xs, zs, acts = layer_forward(meta_of(tick - here), block, *near, xs, zs, acts)
        if tick < ticks - 1:
            near = settle(own, other, block)
            block = lax.ppermute(block, "section", upward)

    every = lax.all_gather(acts[:micro], WIDE, axis=0, tiled=False)

    near = settle(own, other, upstream)
    grad = upstream[0]
    for tick in range(ticks):
        if 0 < tick < micro:
            grad = jnp.where(here == SECTIONS - 1, upstream[tick], grad)
        grad, dzs = layer_backward(meta_of(tick - (SECTIONS - 1 - here)), grad, xs, zs, *near, dzs)
        if tick < ticks - 1:
            near = settle(own, other, grad)
            grad = lax.ppermute(grad, "section", downward)

    members = LOW * ACROSS * CORES
    piece = width // members
    rows = micro * length
    mine = dzs[:micro].reshape(rows, members, piece).transpose(1, 0, 2)
    theirs = lax.all_to_all(mine, WIDE, 0, 0, tiled=True)
    theirs = theirs.reshape(members * micro, length, piece)
    sides = jnp.concatenate([theirs, advanced(theirs, hours)], axis=-1).reshape(members * rows, 2 * piece)
    partial = lax.dot_general(
        every.reshape(members * rows, width), sides, (((0,), (0,)), ((), ())), preferred_element_type=jnp.float32
    ).astype(jnp.bfloat16)
    spread = lax.all_to_all(partial.reshape(HIGH, members * OWN, 2 * piece), "zh", 0, 0, tiled=True)
    total = jnp.sum(spread.astype(jnp.float32), axis=0)
    back = lax.all_to_all(total.reshape(members, OWN, 2 * piece), WIDE, 0, 0, tiled=True)
    owned = back.reshape(members, OWN, 2, piece).transpose(2, 1, 0, 3).reshape(2, OWN, width)
    return owned[None]


def solution(mesh):
    fine = Mesh(mesh.devices.reshape(SECTIONS, HIGH, LOW, ACROSS, CORES), ("section",) + SHARD)
    placed = (
        P(None, SHARD, None, None),
        P(None, SHARD),
        P(),
        P("section"),
        P("section", None, SHARD, None),
        P(None, SHARD, None, None),
    )
    return jax.shard_map(
        shards, mesh=fine, in_specs=placed, out_specs=P("section", None, SHARD, None), check_vma=False
    )
```

time: 523 us -> 391 us (0.75)
  waiting for transfers between devices: 224 us -> 118 us
  local copies, waits for them, and re-layouts: 70.9 us -> 6.57 us
  Pallas kernels: 80.4 us -> 126 us
  blocking collectives: 61.1 us -> 52 us
    unnamed x40 -> x6, local copies, waits for them, and re-layouts: 66.5 us -> 0.02 us
    all_gather x2, waiting for transfers between devices: 132 us -> 74.3 us  [the longest x1 74.3 us: shards(): own = lax.all_gather(row, DEEP, axis=0, tiled=True)]
    pallas_call x18 -> x36, Pallas kernels: 80.4 us -> 126 us  [the longest x18 69 us: settle(): pl.pallas_call(settle_body, out_shape=(pltpu.VMEM(own.shape, own.dtype),...]
    ppermute x8, waiting for transfers between devices: 56.1 us -> 27.6 us  [shards(): grad = lax.ppermute(grad, 'section', downward)]
    ppermute x8, waiting for transfers between devices: 26.6 us -> 0.57 us  [shards(): block = lax.ppermute(block, 'section', upward)]
    all_to_all x2 -> x3, blocking collectives: 61.1 us -> 52 us  [the longest x1 27.2 us: shards(): lax.all_to_all(partial.reshape(HIGH, members * OWN, 2 * piece), 'zh', 0,...]
  transfers between devices with their start and end apart: 19 -> 20, of which waited for: 18 -> 12; matrix products, arithmetic and copies ran while one was open for 1% -> 2% of each run, Pallas kernels for 8% -> 25%
where the time goes in v2:
time: 391 us; the launch traced here: 390 us
  Pallas kernels  126 us (32%)
  waiting for transfers between devices  118 us (30%)
  starting transfers between devices  62.3 us (16%)
  blocking collectives  52 us (13%)
  between operations  14.9 us (4%)
  matrix products  7.25 us (2%)
  local copies, waits for them, and re-layouts  6.57 us (2%)
    all_gather x1, waiting for transfers between devices, shards(): own = lax.all_gather(row, DEEP, axis=0, tiled=True)  74.3 us
    pallas_call x18, Pallas kernels, settle(): pl.pallas_call(settle_body, out_shape=(pltpu.VMEM(own.shape, own.dtype),...  69 us
    ppermute x8, starting transfers between devices, shards(): block = lax.ppermute(block, 'section', upward)  39.8 us
    pallas_call x9, Pallas kernels, layer_backward(): pl.pallas_call(backward_body, out_shape=tuple((jax.ShapeDtypeStruct(v.sha...  33.7 us
    ppermute x8, waiting for transfers between devices, shards(): grad = lax.ppermute(grad, 'section', downward)  27.6 us
    all_to_all x1, blocking collectives, shards(): lax.all_to_all(partial.reshape(HIGH, members * OWN, 2 * piece), 'zh', 0,...  27.2 us
    pallas_call x9, Pallas kernels, layer_forward(): pl.pallas_call(forward_body, out_shape=tuple((jax.ShapeDtypeStruct(v.shap...  23 us
    ppermute x8, starting transfers between devices, shards(): grad = lax.ppermute(grad, 'section', downward)  15.6 us
  transfers between devices with their start and end apart: 20, of which 12 were waited for; matrix products, arithmetic and copies ran while one was open for 2% of the time, Pallas kernels for 25%

profile of v2, /device:TPU:24, one launch (start us, length us, event | category | flops | bytes accessed | tf_op | source)
XLA Modules:
  0.0 390.1 jit_solution(10051421407579570250)
XLA Ops:
  7.5 13.1 %all_to_all.27 = bf16[8,16,1536]{2,1,0:T(8,128)(2,1)} all-to-all(bf16[8,16,1536]{2,1,0:T(8,128)(2,1)S(1)} %bitcast.59), channel_id=1, replica_groups=mesh['section'=8,'zh'=4,'zl'=3,'x'=4,'core'=2] {'x','core'}, dimensions={0} | all-to-all | bytes 786432 | tf_op jit(solution)/shard_map/all_to_all | solution.py:150
  20.7 74.3 %all-gather.4.cloned.1.call-done.own_in = bf16[1536,1536]{1,0:T(8,128)(2,1)} async-done(((bf16[128,1536]{1,0:T(8,128)(2,1)}), bf16[1536,1536]{1,0:T(8,128)(2,1)}) %all-gather.4.cloned.1.call-update) | async-done | bytes 4718608 | tf_op jit(solution)/shard_map/all_gather | solution.py:151
  100.7 4.4 %collective-permute-done.other_in = bf16[1536,1536]{1,0:T(8,128)(2,1)} collective-permute-done((bf16[1536,1536]{1,0:T(8,128)(2,1)}, bf16[1536,1536]{1,0:T(8,128)(2,1)}, u32[]{:S(2)}, u32[]{:S(2)}) %collective-permute-start) | collective-permute-done | bytes 4718624 | tf_op jit(solution)/shard_map/ppermute | solution.py:152
  105.2 3.8 settle.18
  109.2 2.5 layer_forward.9
  111.7 4.6 %collective-permute-start.1 = (bf16[64,1536]{1,0:T(8,128)(2,1)S(1)}, bf16[64,1536]{1,0:T(8,128)(2,1)S(1)}, u32[]{:S(2)}, u32[]{:S(2)}) collective-permute-start(bf16[64,1536]{1,0:T(8,128)(2,1)S(1)} %get-tuple-element.95.after), channel_id=1, source_target_pairs={{0,96},{96,192},{192,288},{288,384},{384,480},{480,576},{576,672},... | collective-permute-start | bytes 589832 | tf_op jit(solution)/shard_map/ppermute | solution.py:176
  116.4 3.8 settle.19
  120.7 2.5 layer_forward.10
  123.2 5.6 %collective-permute-start.2 = (bf16[64,1536]{1,0:T(8,128)(2,1)S(1)}, bf16[64,1536]{1,0:T(8,128)(2,1)S(1)}, u32[]{:S(2)}, u32[]{:S(2)}) collective-permute-start(bf16[64,1536]{1,0:T(8,128)(2,1)S(1)} %get-tuple-element.101.after), channel_id=1, source_target_pairs={{0,96},{96,192},{192,288},{288,384},{384,480},{480,576},{576,672},... | collective-permute-start | bytes 589832 | tf_op jit(solution)/shard_map/ppermute | solution.py:176
  128.9 3.8 settle.20
  132.7 2.5 layer_forward.11
  135.2 5.3 %collective-permute-start.3 = (bf16[64,1536]{1,0:T(8,128)(2,1)S(1)}, bf16[64,1536]{1,0:T(8,128)(2,1)S(1)}, u32[]{:S(2)}, u32[]{:S(2)}) collective-permute-start(bf16[64,1536]{1,0:T(8,128)(2,1)S(1)} %get-tuple-element.107.after), channel_id=1, source_target_pairs={{0,96},{96,192},{192,288},{288,384},{384,480},{480,576},{576,672},... | collective-permute-start | bytes 589832 | tf_op jit(solution)/shard_map/ppermute | solution.py:176
  140.6 3.8 settle.21
  144.4 2.5 layer_forward.12
  146.9 4.9 %collective-permute-start.4 = (bf16[64,1536]{1,0:T(8,128)(2,1)S(1)}, bf16[64,1536]{1,0:T(8,128)(2,1)S(1)}, u32[]{:S(2)}, u32[]{:S(2)}) collective-permute-start(bf16[64,1536]{1,0:T(8,128)(2,1)S(1)} %get-tuple-element.113.after), channel_id=1, source_target_pairs={{0,96},{96,192},{192,288},{288,384},{384,480},{480,576},{576,672},... | collective-permute-start | bytes 589832 | tf_op jit(solution)/shard_map/ppermute | solution.py:176
  151.9 3.8 settle.22
  155.7 2.5 layer_forward.13
  158.2 4.9 %collective-permute-start.5 = (bf16[64,1536]{1,0:T(8,128)(2,1)S(1)}, bf16[64,1536]{1,0:T(8,128)(2,1)S(1)}, u32[]{:S(2)}, u32[]{:S(2)}) collective-permute-start(bf16[64,1536]{1,0:T(8,128)(2,1)S(1)} %get-tuple-element.119.after), channel_id=1, source_target_pairs={{0,96},{96,192},{192,288},{288,384},{384,480},{480,576},{576,672},... | collective-permute-start | bytes 589832 | tf_op jit(solution)/shard_map/ppermute | solution.py:176
  163.1 3.8 settle.23
  167.0 2.5 layer_forward.14
  169.4 4.9 %collective-permute-start.6 = (bf16[64,1536]{1,0:T(8,128)(2,1)S(1)}, bf16[64,1536]{1,0:T(8,128)(2,1)S(1)}, u32[]{:S(2)}, u32[]{:S(2)}) collective-permute-start(bf16[64,1536]{1,0:T(8,128)(2,1)S(1)} %get-tuple-element.125.after), channel_id=1, source_target_pairs={{0,96},{96,192},{192,288},{288,384},{384,480},{480,576},{576,672},... | collective-permute-start | bytes 589832 | tf_op jit(solution)/shard_map/ppermute | solution.py:176
  174.4 3.8 settle.24
  178.2 2.5 layer_forward.15
  180.7 5.0 %collective-permute-start.7 = (bf16[64,1536]{1,0:T(8,128)(2,1)S(1)}, bf16[64,1536]{1,0:T(8,128)(2,1)S(1)}, u32[]{:S(2)}, u32[]{:S(2)}) collective-permute-start(bf16[64,1536]{1,0:T(8,128)(2,1)S(1)} %get-tuple-element.131.after), channel_id=1, source_target_pairs={{0,96},{96,192},{192,288},{288,384},{384,480},{480,576},{576,672},... | collective-permute-start | bytes 589832 | tf_op jit(solution)/shard_map/ppermute | solution.py:176
  185.8 3.8 settle.25
  189.7 2.5 layer_forward.16
  192.1 4.7 %collective-permute-start.8 = (bf16[64,1536]{1,0:T(8,128)(2,1)S(1)}, bf16[64,1536]{1,0:T(8,128)(2,1)S(1)}, u32[]{:S(2)}, u32[]{:S(2)}) collective-permute-start(bf16[64,1536]{1,0:T(8,128)(2,1)S(1)} %get-tuple-element.137.after), channel_id=1, source_target_pairs={{0,96},{96,192},{192,288},{288,384},{384,480},{480,576},{576,672},... | collective-permute-start | bytes 589832 | tf_op jit(solution)/shard_map/ppermute | solution.py:176
  196.9 3.8 settle.26
  200.7 3.2 layer_forward.17
  204.8 3.8 settle.27
  208.7 3.7 layer_backward.9
  212.3 1.9 collective-permute-start.9
  214.4 3.8 settle.28
  218.2 3.0 collective-permute-done.9
  221.1 3.7 layer_backward.10
  226.8 4.0 %settle.29 = (bf16[1536,1536]{1,0:T(8,128)(2,1)S(1)}, bf16[1536,1536]{1,0:T(8,128)(2,1)S(1)}) custom-call(bf16[1536,1536]{1,0:T(8,128)(2,1)} %all-gather.4.cloned.1.call-done.own_in, bf16[1536,1536]{1,0:T(8,128)(2,1)} %collective-permute-done.other_in, bf16[64,1536]{1,0:T(8,128)(2,1)S(1)} %get-tuple-element.152.after), custom_call_target="tpu_custom_call" | custom-call | bytes 18874368 | tf_op jit(solution)/shard_map/settle/pallas_call | solution.py:45
  230.8 3.3 collective-permute-done.10.g_ref
  234.1 3.7 layer_backward.11
  239.8 3.8 settle.30
  243.6 4.2 %collective-permute-done.11.g_ref = bf16[64,1536]{1,0:T(8,128)(2,1)S(1)} collective-permute-done((bf16[64,1536]{1,0:T(8,128)(2,1)S(1)}, bf16[64,1536]{1,0:T(8,128)(2,1)S(1)}, u32[]{:S(2)}, u32[]{:S(2)}) %collective-permute-start.11) | collective-permute-done | bytes 196640 | tf_op jit(solution)/shard_map/ppermute | solution.py:188
  247.8 3.7 layer_backward.12
  251.5 1.9 collective-permute-start.12
  253.5 4.0 %settle.31 = (bf16[1536,1536]{1,0:T(8,128)(2,1)S(1)}, bf16[1536,1536]{1,0:T(8,128)(2,1)S(1)}) custom-call(bf16[1536,1536]{1,0:T(8,128)(2,1)} %all-gather.4.cloned.1.call-done.own_in, bf16[1536,1536]{1,0:T(8,128)(2,1)} %collective-permute-done.other_in, bf16[64,1536]{1,0:T(8,128)(2,1)S(1)} %get-tuple-element.160.after), custom_call_target="tpu_custom_call" | custom-call | bytes 18874368 | tf_op jit(solution)/shard_map/settle/pallas_call | solution.py:45
  257.5 4.6 %collective-permute-done.12.g_ref = bf16[64,1536]{1,0:T(8,128)(2,1)S(1)} collective-permute-done((bf16[64,1536]{1,0:T(8,128)(2,1)S(1)}, bf16[64,1536]{1,0:T(8,128)(2,1)S(1)}, u32[]{:S(2)}, u32[]{:S(2)}) %collective-permute-start.12) | collective-permute-done | bytes 196640 | tf_op jit(solution)/shard_map/ppermute | solution.py:188
  262.1 3.7 layer_backward.13
  265.7 2.1 collective-permute-start.13
  268.0 3.8 settle.32
  271.8 3.8 collective-permute-done.13.g_ref
  275.6 3.7 layer_backward.14
  281.2 4.0 %settle.33 = (bf16[1536,1536]{1,0:T(8,128)(2,1)S(1)}, bf16[1536,1536]{1,0:T(8,128)(2,1)S(1)}) custom-call(bf16[1536,1536]{1,0:T(8,128)(2,1)} %all-gather.4.cloned.1.call-done.own_in, bf16[1536,1536]{1,0:T(8,128)(2,1)} %collective-permute-done.other_in, bf16[64,1536]{1,0:T(8,128)(2,1)S(1)} %get-tuple-element.168.after), custom_call_target="tpu_custom_call" | custom-call | bytes 18874368 | tf_op jit(solution)/shard_map/settle/pallas_call | solution.py:45
  285.2 3.1 collective-permute-done.14.g_ref
  288.3 3.7 layer_backward.15
  292.0 1.9 collective-permute-start.15
  294.0 3.8 settle.34
  297.8 3.0 collective-permute-done.15.g_ref
  300.7 3.7 layer_backward.16
  306.4 4.0 %settle.35 = (bf16[1536,1536]{1,0:T(8,128)(2,1)S(1)}, bf16[1536,1536]{1,0:T(8,128)(2,1)S(1)}) custom-call(bf16[1536,1536]{1,0:T(8,128)(2,1)} %all-gather.4.cloned.1.call-done.own_in, bf16[1536,1536]{1,0:T(8,128)(2,1)} %collective-permute-done.other_in, bf16[64,1536]{1,0:T(8,128)(2,1)S(1)} %get-tuple-element.176.after), custom_call_target="tpu_custom_call" | custom-call | bytes 18874368 | tf_op jit(solution)/shard_map/settle/pallas_call | solution.py:45
  310.4 2.8 collective-permute-done.16.g_ref
  313.2 4.4 %layer_backward.17 = (bf16[64,1536]{1,0:T(8,128)(2,1)}, bf16[3,64,1536]{2,1,0:T(8,128)(2,1)S(1)}) custom-call(s32[3]{0:T(128)S(1)} %add_add_fusion.9.meta, bf16[64,1536]{1,0:T(8,128)(2,1)S(1)} %collective-permute-done.16.g_ref, bf16[3,64,1536]{2,1,0:T(8,128)(2,1)S(1)} %get-tuple-element.144.xs, ...), custom_call_target="tpu_custom_call", output_to_operand_aliasing={{1}: (6, {})} | custom-call | tf_op jit(solution)/shard_map/layer_backward/pallas_call | solution.py:121
  319.3 4.9 %all-to-all-start.1 = ((bf16[24,128,64]{1,2,0:T(8,128)(2,1)}), bf16[24,128,64]{1,2,0:T(8,128)(2,1)S(1)}, u32[]{:S(2)}, u32[]{:S(2)}) async-start(bf16[24,128,64]{1,2,0:T(8,128)(2,1)} %copy.48), calls=%async_computation.1 | async-start | bytes 786432 | tf_op jit(solution)/shard_map/all_to_all | solution.py:194
  324.2 10.8 %all-to-all-done.1 = bf16[24,128,64]{1,2,0:T(8,128)(2,1)S(1)} async-done(((bf16[24,128,64]{1,2,0:T(8,128)(2,1)}), bf16[24,128,64]{1,2,0:T(8,128)(2,1)S(1)}, u32[]{:S(2)}, u32[]{:S(2)}) %all-to-all-start.1) | async-done | bytes 393248 | tf_op jit(solution)/shard_map/all_to_all | solution.py:194
  336.6 6.4 %convolution_convert_fusion = bf16[1536,128]{1,0:T(8,128)(2,1)S(1)} fusion(bf16[3072,1536]{1,0:T(8,128)(2,1)} %bitcast.64, bf16[3072,64]{0,1:T(8,128)(2,1)S(1)} %concatenate.13, bf16[3072,64]{0,1:T(8,128)(2,1)S(1)} %copy_bitcast_fusion), kind=kOutput, calls=%fused_computation | convolution fusion | flops 1209729024 | bytes 10616832 | tf_op jit(solution)/shard_map/dot_general | solution.py:197
  343.0 27.2 %all_to_all.28 = bf16[4,384,128]{2,1,0:T(8,128)(2,1)S(1)} all-to-all(bf16[4,384,128]{2,1,0:T(8,128)(2,1)S(1)} %bitcast.61), channel_id=1, replica_groups=mesh['section'=8,'zh'=4,'zl'=3,'x'=4,'core'=2] {'zh'}, dimensions={0} | all-to-all | bytes 786432 | tf_op jit(solution)/shard_map/all_to_all | solution.py:200
  370.3 11.7 %all_to_all.29 = f32[24,16,128]{2,1,0:T(8,128)S(1)} all-to-all(f32[24,16,128]{2,1,0:T(8,128)S(1)} %bitcast.60), channel_id=1, replica_groups=mesh['section'=8,'zh'=4,'zl'=3,'x'=4,'core'=2] {'zl','x','core'}, dimensions={0} | all-to-all | bytes 393216 | tf_op jit(solution)/shard_map/all_to_all | solution.py:202
  (67 shorter events, 21.3 us)
Async XLA Ops:
  6.5 91.1 %copy-start = (bf16[128,1536]{1,0:T(8,128)(2,1)S(1)}, bf16[128,1536]{1,0:T(8,128)(2,1)}, u32[]{:S(2)}) copy-start(bf16[128,1536]{1,0:T(8,128)(2,1)} %param.8) | copy-start | bytes 1179652
  6.5 88.5 %all-gather.4.cloned.1.call-start = ((), (), s32[]{:S(2)}) async-start(), calls=%async_computation.4 | async-start | bytes 5111808 | tf_op jit(solution)/shard_map/all_gather | solution.py:151
  20.7 315.9 %all-gather.6.cloned.1.call-start = ((), (), s32[]{:S(2)}) async-start(), calls=%async_computation.5 | async-start | bytes 9830400 | tf_op jit(solution)/shard_map/all_gather | solution.py:178
  95.0 10.1 %collective-permute-start = (bf16[1536,1536]{1,0:T(8,128)(2,1)}, bf16[1536,1536]{1,0:T(8,128)(2,1)}, u32[]{:S(2)}, u32[]{:S(2)}) collective-permute-start(bf16[1536,1536]{1,0:T(8,128)(2,1)} %all-gather.4.cloned.1.call-done.own_in), channel_id=1, source_target_pairs={{0,1},{1,0},{2,3},{3,2},{4,5},{5,4},{6,7},{7,6},{8,9},{9,8},{10,11... | collective-permute-start | bytes 14155784 | tf_op jit(solution)/shard_map/ppermute | solution.py:152
  111.7 9.1 %collective-permute-start.1 = (bf16[64,1536]{1,0:T(8,128)(2,1)S(1)}, bf16[64,1536]{1,0:T(8,128)(2,1)S(1)}, u32[]{:S(2)}, u32[]{:S(2)}) collective-permute-start(bf16[64,1536]{1,0:T(8,128)(2,1)S(1)} %get-tuple-element.95.after), channel_id=1, source_target_pairs={{0,96},{96,192},{192,288},{288,384},{384,480},{480,576},{576,672},... | collective-permute-start | bytes 589832 | tf_op jit(solution)/shard_map/ppermute | solution.py:176
  123.2 9.5 %collective-permute-start.2 = (bf16[64,1536]{1,0:T(8,128)(2,1)S(1)}, bf16[64,1536]{1,0:T(8,128)(2,1)S(1)}, u32[]{:S(2)}, u32[]{:S(2)}) collective-permute-start(bf16[64,1536]{1,0:T(8,128)(2,1)S(1)} %get-tuple-element.101.after), channel_id=1, source_target_pairs={{0,96},{96,192},{192,288},{288,384},{384,480},{480,576},{576,672},... | collective-permute-start | bytes 589832 | tf_op jit(solution)/shard_map/ppermute | solution.py:176
  135.2 9.2 %collective-permute-start.3 = (bf16[64,1536]{1,0:T(8,128)(2,1)S(1)}, bf16[64,1536]{1,0:T(8,128)(2,1)S(1)}, u32[]{:S(2)}, u32[]{:S(2)}) collective-permute-start(bf16[64,1536]{1,0:T(8,128)(2,1)S(1)} %get-tuple-element.107.after), channel_id=1, source_target_pairs={{0,96},{96,192},{192,288},{288,384},{384,480},{480,576},{576,672},... | collective-permute-start | bytes 589832 | tf_op jit(solution)/shard_map/ppermute | solution.py:176
  146.9 8.8 %collective-permute-start.4 = (bf16[64,1536]{1,0:T(8,128)(2,1)S(1)}, bf16[64,1536]{1,0:T(8,128)(2,1)S(1)}, u32[]{:S(2)}, u32[]{:S(2)}) collective-permute-start(bf16[64,1536]{1,0:T(8,128)(2,1)S(1)} %get-tuple-element.113.after), channel_id=1, source_target_pairs={{0,96},{96,192},{192,288},{288,384},{384,480},{480,576},{576,672},... | collective-permute-start | bytes 589832 | tf_op jit(solution)/shard_map/ppermute | solution.py:176
  158.2 8.8 %collective-permute-start.5 = (bf16[64,1536]{1,0:T(8,128)(2,1)S(1)}, bf16[64,1536]{1,0:T(8,128)(2,1)S(1)}, u32[]{:S(2)}, u32[]{:S(2)}) collective-permute-start(bf16[64,1536]{1,0:T(8,128)(2,1)S(1)} %get-tuple-element.119.after), channel_id=1, source_target_pairs={{0,96},{96,192},{192,288},{288,384},{384,480},{480,576},{576,672},... | collective-permute-start | bytes 589832 | tf_op jit(solution)/shard_map/ppermute | solution.py:176
  169.4 8.8 %collective-permute-start.6 = (bf16[64,1536]{1,0:T(8,128)(2,1)S(1)}, bf16[64,1536]{1,0:T(8,128)(2,1)S(1)}, u32[]{:S(2)}, u32[]{:S(2)}) collective-permute-start(bf16[64,1536]{1,0:T(8,128)(2,1)S(1)} %get-tuple-element.125.after), channel_id=1, source_target_pairs={{0,96},{96,192},{192,288},{288,384},{384,480},{480,576},{576,672},... | collective-permute-start | bytes 589832 | tf_op jit(solution)/shard_map/ppermute | solution.py:176
  180.7 8.9 %collective-permute-start.7 = (bf16[64,1536]{1,0:T(8,128)(2,1)S(1)}, bf16[64,1536]{1,0:T(8,128)(2,1)S(1)}, u32[]{:S(2)}, u32[]{:S(2)}) collective-permute-start(bf16[64,1536]{1,0:T(8,128)(2,1)S(1)} %get-tuple-element.131.after), channel_id=1, source_target_pairs={{0,96},{96,192},{192,288},{288,384},{384,480},{480,576},{576,672},... | collective-permute-start | bytes 589832 | tf_op jit(solution)/shard_map/ppermute | solution.py:176
  192.1 8.6 %collective-permute-start.8 = (bf16[64,1536]{1,0:T(8,128)(2,1)S(1)}, bf16[64,1536]{1,0:T(8,128)(2,1)S(1)}, u32[]{:S(2)}, u32[]{:S(2)}) collective-permute-start(bf16[64,1536]{1,0:T(8,128)(2,1)S(1)} %get-tuple-element.137.after), channel_id=1, source_target_pairs={{0,96},{96,192},{192,288},{288,384},{384,480},{480,576},{576,672},... | collective-permute-start | bytes 589832 | tf_op jit(solution)/shard_map/ppermute | solution.py:176
  200.7 4.1 %copy-start.2 = (bf16[2,1,64,1536]{3,2,1,0:T(8,128)(2,1)S(1)}, bf16[2,1,64,1536]{3,2,1,0:T(8,128)(2,1)}, u32[]{:S(2)}) copy-start(bf16[2,1,64,1536]{3,2,1,0:T(8,128)(2,1)} %param.11) | copy-start | bytes 1179652
  212.3 8.8 %collective-permute-start.9 = (bf16[64,1536]{1,0:T(8,128)(2,1)S(1)}, bf16[64,1536]{1,0:T(8,128)(2,1)S(1)}, u32[]{:S(2)}, u32[]{:S(2)}) collective-permute-start(bf16[64,1536]{1,0:T(8,128)(2,1)S(1)} %get-tuple-element.148.after), channel_id=1, source_target_pairs={{96,0},{192,96},{288,192},{384,288},{480,384},{576,480},{672,576},... | collective-permute-start | bytes 589832 | tf_op jit(solution)/shard_map/ppermute | solution.py:188
  224.8 9.3 %collective-permute-start.10 = (bf16[64,1536]{1,0:T(8,128)(2,1)S(1)}, bf16[64,1536]{1,0:T(8,128)(2,1)S(1)}, u32[]{:S(2)}, u32[]{:S(2)}) collective-permute-start(bf16[64,1536]{1,0:T(8,128)(2,1)S(1)} %get-tuple-element.152.after), channel_id=1, source_target_pairs={{96,0},{192,96},{288,192},{384,288},{480,384},{576,480},{672,576},... | collective-permute-start | bytes 589832 | tf_op jit(solution)/shard_map/ppermute | solution.py:188
  237.8 10.0 %collective-permute-start.11 = (bf16[64,1536]{1,0:T(8,128)(2,1)S(1)}, bf16[64,1536]{1,0:T(8,128)(2,1)S(1)}, u32[]{:S(2)}, u32[]{:S(2)}) collective-permute-start(bf16[64,1536]{1,0:T(8,128)(2,1)S(1)} %get-tuple-element.156.after), channel_id=1, source_target_pairs={{96,0},{192,96},{288,192},{384,288},{480,384},{576,480},{672,576},... | collective-permute-start | bytes 589832 | tf_op jit(solution)/shard_map/ppermute | solution.py:188
  251.5 10.6 %collective-permute-start.12 = (bf16[64,1536]{1,0:T(8,128)(2,1)S(1)}, bf16[64,1536]{1,0:T(8,128)(2,1)S(1)}, u32[]{:S(2)}, u32[]{:S(2)}) collective-permute-start(bf16[64,1536]{1,0:T(8,128)(2,1)S(1)} %get-tuple-element.160.after), channel_id=1, source_target_pairs={{96,0},{192,96},{288,192},{384,288},{480,384},{576,480},{672,576},... | collective-permute-start | bytes 589832 | tf_op jit(solution)/shard_map/ppermute | solution.py:188
  265.7 9.8 %collective-permute-start.13 = (bf16[64,1536]{1,0:T(8,128)(2,1)S(1)}, bf16[64,1536]{1,0:T(8,128)(2,1)S(1)}, u32[]{:S(2)}, u32[]{:S(2)}) collective-permute-start(bf16[64,1536]{1,0:T(8,128)(2,1)S(1)} %get-tuple-element.164.after), channel_id=1, source_target_pairs={{96,0},{192,96},{288,192},{384,288},{480,384},{576,480},{672,576},... | collective-permute-start | bytes 589832 | tf_op jit(solution)/shard_map/ppermute | solution.py:188
  279.2 9.1 %collective-permute-start.14 = (bf16[64,1536]{1,0:T(8,128)(2,1)S(1)}, bf16[64,1536]{1,0:T(8,128)(2,1)S(1)}, u32[]{:S(2)}, u32[]{:S(2)}) collective-permute-start(bf16[64,1536]{1,0:T(8,128)(2,1)S(1)} %get-tuple-element.168.after), channel_id=1, source_target_pairs={{96,0},{192,96},{288,192},{384,288},{480,384},{576,480},{672,576},... | collective-permute-start | bytes 589832 | tf_op jit(solution)/shard_map/ppermute | solution.py:188
  292.0 8.8 %collective-permute-start.15 = (bf16[64,1536]{1,0:T(8,128)(2,1)S(1)}, bf16[64,1536]{1,0:T(8,128)(2,1)S(1)}, u32[]{:S(2)}, u32[]{:S(2)}) collective-permute-start(bf16[64,1536]{1,0:T(8,128)(2,1)S(1)} %get-tuple-element.172.after), channel_id=1, source_target_pairs={{96,0},{192,96},{288,192},{384,288},{480,384},{576,480},{672,576},... | collective-permute-start | bytes 589832 | tf_op jit(solution)/shard_map/ppermute | solution.py:188
  304.4 8.8 %collective-permute-start.16 = (bf16[64,1536]{1,0:T(8,128)(2,1)S(1)}, bf16[64,1536]{1,0:T(8,128)(2,1)S(1)}, u32[]{:S(2)}, u32[]{:S(2)}) collective-permute-start(bf16[64,1536]{1,0:T(8,128)(2,1)S(1)} %get-tuple-element.176.after), channel_id=1, source_target_pairs={{96,0},{192,96},{288,192},{384,288},{480,384},{576,480},{672,576},... | collective-permute-start | bytes 589832 | tf_op jit(solution)/shard_map/ppermute | solution.py:188
  319.3 15.8 %all-to-all-start.1 = ((bf16[24,128,64]{1,2,0:T(8,128)(2,1)}), bf16[24,128,64]{1,2,0:T(8,128)(2,1)S(1)}, u32[]{:S(2)}, u32[]{:S(2)}) async-start(bf16[24,128,64]{1,2,0:T(8,128)(2,1)} %copy.48), calls=%async_computation.1 | async-start | bytes 786432 | tf_op jit(solution)/shard_map/all_to_all | solution.py:194
  336.6 46.7 %copy-start.1 = (bf16[128,1536]{1,0:T(8,128)(2,1)S(1)}, bf16[128,1536]{1,0:T(8,128)(2,1)}, u32[]{:S(2)}) copy-start(bf16[128,1536]{1,0:T(8,128)(2,1)} %param.8) | copy-start | bytes 1179652
Sparse Core Ops, SparseCore 0:
  20.8 74.1 all-gather.3
  204.8 112.8 all-gather.5

commit v3 on v2

--- a/solution.py
+++ b/solution.py
@@ -28,11 +28,11 @@
     return inverse, x_full * inverse
 
 
-def settle_body(own_in, other_in, after, own, other, sems):
-    del after
+def settle_body(*refs):
+    count = (len(refs) - 2) // 2
+    sems = refs[-1]
     copies = [
-        pltpu.make_async_copy(own_in, own, sems.at[0]),
-        pltpu.make_async_copy(other_in, other, sems.at[1]),
+        pltpu.make_async_copy(refs[i], refs[count + 1 + i], sems.at[i]) for i in range(count)
     ]
     for copy in copies:
         copy.start()
@@ -40,18 +40,18 @@
         copy.wait()
 
 
-def settle(own, other, after):
-    size = own.size * own.dtype.itemsize
+def settle(arrays, after):
+    size = sum(v.size * v.dtype.itemsize for v in arrays)
     return pl.pallas_call(
         settle_body,
-        out_shape=(pltpu.VMEM(own.shape, own.dtype), pltpu.VMEM(other.shape, other.dtype)),
-        in_specs=[pl.BlockSpec(memory_space=pltpu.HBM)] * 2 + [pl.BlockSpec(memory_space=pl.ANY)],
-        out_specs=[pl.BlockSpec(memory_space=pltpu.VMEM)] * 2,
-        scratch_shapes=[pltpu.SemaphoreType.DMA((2,))],
+        out_shape=tuple(pltpu.VMEM(v.shape, v.dtype) for v in arrays),
+        in_specs=[pl.BlockSpec(memory_space=pltpu.HBM)] * len(arrays) + [pl.BlockSpec(memory_space=pl.ANY)],
+        out_specs=tuple(VMEM for _ in arrays),
+        scratch_shapes=[pltpu.SemaphoreType.DMA((len(arrays),))],
         cost_estimate=pl.CostEstimate(flops=0, transcendentals=0, bytes_accessed=4 * size),
         compiler_params=pltpu.CompilerParams(vmem_limit_bytes=LIMIT),
         name="settle",
-    )(pltpu.with_memory_space_constraint(own, pltpu.HBM), pltpu.with_memory_space_constraint(other, pltpu.HBM), after)
+    )(*(pltpu.with_memory_space_constraint(v, pltpu.HBM) for v in arrays), after)
 
 
 def ordered(meta, current, moved):
@@ -61,8 +61,7 @@
     return first, second
 
 
-def forward_body(meta, x_ref, own_ref, other_ref, keep_x, keep_z, keep_a, x_out, xs, zs, acts):
-    del keep_x, keep_z, keep_a
+def forward_part(meta, x_ref, own_ref, other_ref, x_out, xs, zs, acts):
     slot = meta[0]
     x_full = x_ref[...].astype(jnp.float32)
     _, normed = norm_of(x_full)
@@ -79,25 +78,8 @@
         x_out[:, cols] = (x_ref[:, cols].astype(jnp.float32) + pre * jax.nn.sigmoid(pre)).astype(jnp.bfloat16)
 
 
-VMEM = pl.BlockSpec(memory_space=pltpu.VMEM)
-SMEM = pl.BlockSpec(memory_space=pltpu.SMEM)
-
-
-def layer_forward(meta, x_in, own, other, xs, zs, acts):
-    return pl.pallas_call(
-        forward_body,
-        out_shape=tuple(jax.ShapeDtypeStruct(v.shape, v.dtype) for v in (x_in, xs, zs, acts)),
-        in_specs=[SMEM] + [VMEM] * 6,
-        out_specs=[VMEM] * 4,
-        input_output_aliases={4: 1, 5: 2, 6: 3},
-        compiler_params=pltpu.CompilerParams(vmem_limit_bytes=LIMIT),
-        name="layer_forward",
-    )(meta, x_in, own, other, xs, zs, acts)
-
-
-def backward_body(meta, g_ref, xs, zs, own_ref, other_ref, keep_d, g_out, dzs, da):
-    del keep_d
-    slot = meta[0]
+def backward_part(meta, g_ref, own_ref, other_ref, xs, zs, g_out, dzs, da):
+    slot = meta[3]
     pre = zs[slot]
     sigma = jax.nn.sigmoid(pre)
     d_pre = g_ref[...].astype(jnp.float32) * sigma * (1.0 + pre * (1.0 - sigma))
@@ -117,17 +99,42 @@
     g_out[...] = (g_ref[...].astype(jnp.float32) + inverse * (d_norm - normed * mean)).astype(jnp.bfloat16)
 
 
-def layer_backward(meta, g_in, xs, zs, own, other, dzs):
+def forward_body(meta, x_ref, own_ref, other_ref, keep_x, keep_z, keep_a, x_out, xs, zs, acts):
+    del keep_x, keep_z, keep_a
+    forward_part(meta, x_ref, own_ref, other_ref, x_out, xs, zs, acts)
+
+
+def backward_body(meta, g_ref, own_ref, other_ref, xs, zs, keep_d, g_out, dzs, da):
+    del keep_d
+    backward_part(meta, g_ref, own_ref, other_ref, xs, zs, g_out, dzs, da)
+
+
+def turn_body(
+    meta, x_ref, g_ref, own_ref, other_ref, keep_x, keep_z, keep_a, keep_d, x_out, g_out, xs, zs, acts, dzs, da
+):
+    del keep_x, keep_z, keep_a, keep_d
+    forward_part(meta, x_ref, own_ref, other_ref, x_out, xs, zs, acts)
+    backward_part(meta, g_ref, own_ref, other_ref, xs, zs, g_out, dzs, da)
+
+
+VMEM = pl.BlockSpec(memory_space=pltpu.VMEM)
+SMEM = pl.BlockSpec(memory_space=pltpu.SMEM)
+
+
+def run(body, name, meta, free, weights, kept, read, scratch):
+    operands = (meta, *free, *weights, *read, *kept)
+    first = len(operands) - len(kept)
     return pl.pallas_call(
-        backward_body,
-        out_shape=tuple(jax.ShapeDtypeStruct(v.shape, v.dtype) for v in (g_in, dzs)),
-        in_specs=[SMEM] + [VMEM] * 6,
-        out_specs=[VMEM] * 2,
-        scratch_shapes=[pltpu.VMEM(g_in.shape, jnp.float32)],
-        input_output_aliases={6: 1},
+        body,
+        out_shape=tuple(jax.ShapeDtypeStruct(v.shape, v.dtype) for v in free)
+        + tuple(pltpu.VMEM(v.shape, v.dtype) for v in kept),
+        in_specs=[SMEM] + [VMEM] * (len(operands) - 1),
+        out_specs=tuple(VMEM for _ in range(len(free) + len(kept))),
+        scratch_shapes=scratch,
+        input_output_aliases={first + i: len(free) + i for i in range(len(kept))},
         compiler_params=pltpu.CompilerParams(vmem_limit_bytes=LIMIT),
-        name="layer_backward",
-    )(meta, g_in, xs, zs, own, other, dzs)
+        name=name,
+    )(*operands)
 
 
 def advanced(values, hours):
@@ -150,7 +157,6 @@
     row = lax.all_to_all(copies, ROW, 0, 0, tiled=True)
     own = lax.all_gather(row, DEEP, axis=0, tiled=True)
     other = lax.ppermute(own, "core", [(0, 1), (1, 0)])
-    near = settle(own, other, inputs)
 
     ticks = SECTIONS + micro - 1
     slots = (micro + 1, length, width)
@@ -158,40 +164,56 @@
     acts = jnp.zeros(slots, jnp.bfloat16)
     zs = jnp.zeros(slots, jnp.float32)
     dzs = jnp.zeros(slots, jnp.bfloat16)
-
-    def meta_of(order):
-        inside = jnp.logical_and(order >= 0, order < micro)
-        return jnp.stack([jnp.where(inside, order, micro), hours, core]).astype(jnp.int32)
+    scratch = [pltpu.VMEM((length, width), jnp.float32)]
+
+    def slot_of(order):
+        return jnp.where(jnp.logical_and(order >= 0, order < micro), order, micro)
+
+    def meta_of(ahead, behind):
+        parts = [slot_of(ahead - here), hours, core, slot_of(behind - (SECTIONS - 1 - here))]
+        return jnp.stack(parts).astype(jnp.int32)
 
     upward = [(i, i + 1) for i in range(SECTIONS - 1)]
     downward = [(i + 1, i) for i in range(SECTIONS - 1)]
 
     block = inputs[0]
-    for tick in range(ticks):
+    grad = upstream[0]
+    near = settle((own,), inputs) + settle((other,), inputs)
+    for tick in range(ticks + SECTIONS - 1):
+        behind = tick - (SECTIONS - 1)
+        meta = meta_of(tick, behind)
         if 0 < tick < micro:
             block = jnp.where(here == 0, inputs[tick], block)
-        block, xs, zs, acts = layer_forward(meta_of(tick - here), block, *near, xs, zs, acts)
+        if 0 < behind < micro:
+            grad = jnp.where(here == SECTIONS - 1, upstream[behind], grad)
+        if behind < 0:
+            block, xs, zs, acts = run(forward_body, "layer_forward", meta, (block,), near, (xs, zs, acts), (), [])
+            lead = block
+        elif tick < ticks:
+            block, grad, xs, zs, acts, dzs = run(
+                turn_body, "layer_turn", meta, (block, grad), near, (xs, zs, acts, dzs), (), scratch
+            )
+            lead = grad
+        else:
+            grad, dzs = run(backward_body, "layer_backward", meta, (grad,), near, (dzs,), (xs, zs), scratch)
+            lead = grad
+        if tick == ticks + 1:
+            every, lead = lax.optimization_barrier((every, lead))
+            every = lax.all_gather(every, ROW, axis=0, tiled=False)
+        if tick < ticks + SECTIONS - 2:
+            near = settle((own, other), lead)
         if tick < ticks - 1:
-            near = settle(own, other, block)
             block = lax.ppermute(block, "section", upward)
-
-    every = lax.all_gather(acts[:micro], WIDE, axis=0, tiled=False)
-
-    near = settle(own, other, upstream)
-    grad = upstream[0]
-    for tick in range(ticks):
-        if 0 < tick < micro:
-            grad = jnp.where(here == SECTIONS - 1, upstream[tick], grad)
-        grad, dzs = layer_backward(meta_of(tick - (SECTIONS - 1 - here)), grad, xs, zs, *near, dzs)
-        if tick < ticks - 1:
-            near = settle(own, other, grad)
+        if 0 <= behind and tick < ticks + SECTIONS - 2:
             grad = lax.ppermute(grad, "section", downward)
+        if tick == ticks - 1:
+            every = lax.all_gather(acts[:micro], "zl", axis=0, tiled=False)
 
     members = LOW * ACROSS * CORES
     piece = width // members
     rows = micro * length
     mine = dzs[:micro].reshape(rows, members, piece).transpose(1, 0, 2)
-    theirs = lax.all_to_all(mine, WIDE, 0, 0, tiled=True)
+    theirs = lax.all_to_all(mine, ROW + ("zl",), 0, 0, tiled=True)
     theirs = theirs.reshape(members * micro, length, piece)
     sides = jnp.concatenate([theirs, advanced(theirs, hours)], axis=-1).reshape(members * rows, 2 * piece)
     partial = lax.dot_general(
@@ -200,7 +222,8 @@
     spread = lax.all_to_all(partial.reshape(HIGH, members * OWN, 2 * piece), "zh", 0, 0, tiled=True)
     total = jnp.sum(spread.astype(jnp.float32), axis=0)
     back = lax.all_to_all(total.reshape(members, OWN, 2 * piece), WIDE, 0, 0, tiled=True)
-    owned = back.reshape(members, OWN, 2, piece).transpose(2, 1, 0, 3).reshape(2, OWN, width)
+    back = back.reshape(LOW, ACROSS * CORES, OWN, 2, piece)
+    owned = back.transpose(3, 2, 1, 0, 4).reshape(2, OWN, width)
     return owned[None]
 
 

time: 391 us -> 390 us (level)
  Pallas kernels: 126 us -> 117 us
    all_gather x1 -> x2, waiting for transfers between devices: 0.02 us -> 11.5 us  [the longest x1 11.5 us: shards(): every = lax.all_gather(acts[:micro], 'zl', axis=0, tiled=False)]
    pallas_call x36 -> x33, Pallas kernels: 126 us -> 117 us  [the longest x17 62.4 us: settle(): pl.pallas_call(settle_body, out_shape=tuple((pltpu.VMEM(v.shape, v.dtype)...]
    ppermute x8, waiting for transfers between devices: 27.6 us -> 19.9 us  [shards(): grad = lax.ppermute(grad, 'section', downward)]
  transfers between devices with their start and end apart: 20 -> 21, of which waited for: 12 -> 12; matrix products, arithmetic and copies ran while one was open for 2% -> 2% of each run, Pallas kernels for 25% -> 22%
where the time goes in v3:
time: 390 us; the launch traced here: 388 us
  waiting for transfers between devices  120 us (31%)
  Pallas kernels  117 us (30%)
  starting transfers between devices  64.2 us (16%)
  blocking collectives  54 us (14%)
  between operations  14.6 us (4%)
  local copies, waits for them, and re-layouts  7.5 us (2%)
  matrix products  7.25 us (2%)
    all_gather x1, waiting for transfers between devices, shards(): own = lax.all_gather(row, DEEP, axis=0, tiled=True)  74.3 us
    pallas_call x17, Pallas kernels, settle(): pl.pallas_call(settle_body, out_shape=tuple((pltpu.VMEM(v.shape, v.dtype)...  62.4 us
    pallas_call x16, Pallas kernels, run(): pl.pallas_call(body, out_shape=tuple((jax.ShapeDtypeStruct(v.shape, v.dty...  54.6 us
    ppermute x8, starting transfers between devices, shards(): block = lax.ppermute(block, 'section', upward)  40.4 us
    all_to_all x1, blocking collectives, shards(): lax.all_to_all(partial.reshape(HIGH, members * OWN, 2 * piece), 'zh', 0,...  29.5 us
    ppermute x8, waiting for transfers between devices, shards(): grad = lax.ppermute(grad, 'section', downward)  19.9 us
    ppermute x8, starting transfers between devices, shards(): grad = lax.ppermute(grad, 'section', downward)  16.1 us
    all_to_all x1, blocking collectives, shards(): row = lax.all_to_all(copies, ROW, 0, 0, tiled=True)  13.1 us
  transfers between devices with their start and end apart: 21, of which 12 were waited for; matrix products, arithmetic and copies ran while one was open for 2% of the time, Pallas kernels for 22%

profile of v3, /device:TPU:24, one launch (start us, length us, event | category | flops | bytes accessed | tf_op | source)
XLA Modules:
  0.0 388.2 jit_solution(18349743695938785853)
XLA Ops:
  7.5 13.1 %all_to_all.27 = bf16[8,16,1536]{2,1,0:T(8,128)(2,1)} all-to-all(bf16[8,16,1536]{2,1,0:T(8,128)(2,1)S(1)} %bitcast.70), channel_id=1, replica_groups=mesh['section'=8,'zh'=4,'zl'=3,'x'=4,'core'=2] {'x','core'}, dimensions={0} | all-to-all | bytes 786432 | tf_op jit(solution)/shard_map/all_to_all | solution.py:157
  20.7 74.3 %all-gather.6.cloned.1.call-done.refs_0_ = bf16[1536,1536]{1,0:T(8,128)(2,1)} async-done(((bf16[128,1536]{1,0:T(8,128)(2,1)}), bf16[1536,1536]{1,0:T(8,128)(2,1)}) %all-gather.6.cloned.1.call-update) | async-done | bytes 4718608 | tf_op jit(solution)/shard_map/all_gather | solution.py:158
  100.7 2.3 settle.17.own_ref
  103.1 2.1 collective-permute-done.refs_0_.refs_1_
  105.2 2.3 settle.18.other_ref
  107.7 2.5 layer_forward.7
  110.2 4.6 %collective-permute-start.1 = (bf16[64,1536]{1,0:T(8,128)(2,1)S(1)}, bf16[64,1536]{1,0:T(8,128)(2,1)S(1)}, u32[]{:S(2)}, u32[]{:S(2)}) collective-permute-start(bf16[64,1536]{1,0:T(8,128)(2,1)S(1)} %get-tuple-element.89.refs_2_), channel_id=1, source_target_pairs={{0,96},{96,192},{192,288},{288,384},{384,480},{480,576},{576,672},... | collective-permute-start | bytes 589832 | tf_op jit(solution)/shard_map/ppermute | solution.py:206
  114.9 3.8 settle.19
  119.3 2.5 layer_forward.8
  121.8 5.6 %collective-permute-start.2 = (bf16[64,1536]{1,0:T(8,128)(2,1)S(1)}, bf16[64,1536]{1,0:T(8,128)(2,1)S(1)}, u32[]{:S(2)}, u32[]{:S(2)}) collective-permute-start(bf16[64,1536]{1,0:T(8,128)(2,1)S(1)} %get-tuple-element.95.refs_2_), channel_id=1, source_target_pairs={{0,96},{96,192},{192,288},{288,384},{384,480},{480,576},{576,672},... | collective-permute-start | bytes 589832 | tf_op jit(solution)/shard_map/ppermute | solution.py:206
  127.5 3.8 settle.20
  131.3 2.4 layer_forward.9
  133.8 5.3 %collective-permute-start.3 = (bf16[64,1536]{1,0:T(8,128)(2,1)S(1)}, bf16[64,1536]{1,0:T(8,128)(2,1)S(1)}, u32[]{:S(2)}, u32[]{:S(2)}) collective-permute-start(bf16[64,1536]{1,0:T(8,128)(2,1)S(1)} %get-tuple-element.101.refs_2_), channel_id=1, source_target_pairs={{0,96},{96,192},{192,288},{288,384},{384,480},{480,576},{576,672},... | collective-permute-start | bytes 589832 | tf_op jit(solution)/shard_map/ppermute | solution.py:206
  139.2 3.8 settle.21
  143.0 2.4 layer_forward.10
  145.4 4.9 %collective-permute-start.4 = (bf16[64,1536]{1,0:T(8,128)(2,1)S(1)}, bf16[64,1536]{1,0:T(8,128)(2,1)S(1)}, u32[]{:S(2)}, u32[]{:S(2)}) collective-permute-start(bf16[64,1536]{1,0:T(8,128)(2,1)S(1)} %get-tuple-element.107.refs_2_), channel_id=1, source_target_pairs={{0,96},{96,192},{192,288},{288,384},{384,480},{480,576},{576,672},... | collective-permute-start | bytes 589832 | tf_op jit(solution)/shard_map/ppermute | solution.py:206
  150.4 3.8 settle.22
  154.2 2.4 layer_forward.11
  156.6 4.9 %collective-permute-start.5 = (bf16[64,1536]{1,0:T(8,128)(2,1)S(1)}, bf16[64,1536]{1,0:T(8,128)(2,1)S(1)}, u32[]{:S(2)}, u32[]{:S(2)}) collective-permute-start(bf16[64,1536]{1,0:T(8,128)(2,1)S(1)} %get-tuple-element.113.refs_2_), channel_id=1, source_target_pairs={{0,96},{96,192},{192,288},{288,384},{384,480},{480,576},{576,672},... | collective-permute-start | bytes 589832 | tf_op jit(solution)/shard_map/ppermute | solution.py:206
  161.6 3.8 settle.23
  165.4 2.4 layer_forward.12
  167.9 4.9 %collective-permute-start.6 = (bf16[64,1536]{1,0:T(8,128)(2,1)S(1)}, bf16[64,1536]{1,0:T(8,128)(2,1)S(1)}, u32[]{:S(2)}, u32[]{:S(2)}) collective-permute-start(bf16[64,1536]{1,0:T(8,128)(2,1)S(1)} %get-tuple-element.119.refs_2_), channel_id=1, source_target_pairs={{0,96},{96,192},{192,288},{288,384},{384,480},{480,576},{576,672},... | collective-permute-start | bytes 589832 | tf_op jit(solution)/shard_map/ppermute | solution.py:206
  172.8 3.8 settle.24
  176.7 2.4 layer_forward.13
  179.1 5.0 %collective-permute-start.7 = (bf16[64,1536]{1,0:T(8,128)(2,1)S(1)}, bf16[64,1536]{1,0:T(8,128)(2,1)S(1)}, u32[]{:S(2)}, u32[]{:S(2)}) collective-permute-start(bf16[64,1536]{1,0:T(8,128)(2,1)S(1)} %get-tuple-element.125.refs_2_), channel_id=1, source_target_pairs={{0,96},{96,192},{192,288},{288,384},{384,480},{480,576},{576,672},... | collective-permute-start | bytes 589832 | tf_op jit(solution)/shard_map/ppermute | solution.py:206
  184.3 3.8 settle.25
  188.1 5.6 %layer_turn.2 = (bf16[64,1536]{1,0:T(8,128)(2,1)S(1)}, bf16[64,1536]{1,0:T(8,128)(2,1)S(1)}, bf16[3,64,1536]{2,1,0:T(8,128)(2,1)S(1)}, f32[3,64,1536]{2,1,0:T(8,...) custom-call(s32[4]{0:T(128)S(1)} %pad_add_fusion.1.meta, ...), custom_call_target="tpu_custom_call", output_to_operand_aliasing={{2}: (5, {}), {3}: (6, {}), {4}: (7, {}), {5}: (8, {})} | custom-call | tf_op jit(solution)/shard_map/layer_turn/pallas_call | solution.py:127
  196.4 5.3 %collective-permute-start.8 = (bf16[64,1536]{1,0:T(8,128)(2,1)}, bf16[64,1536]{1,0:T(8,128)(2,1)S(1)}, u32[]{:S(2)}, u32[]{:S(2)}) collective-permute-start(bf16[64,1536]{1,0:T(8,128)(2,1)} %copy-done.2), channel_id=1, source_target_pairs={{0,96},{96,192},{192,288},{288,384},{384,480},{480,576},{576,672},... | collective-permute-start | bytes 589832 | tf_op jit(solution)/shard_map/ppermute | solution.py:206
  201.7 3.8 settle.26
  205.6 5.5 %layer_turn.3 = (bf16[64,1536]{1,0:T(8,128)(2,1)}, bf16[64,1536]{1,0:T(8,128)(2,1)S(1)}, bf16[3,64,1536]{2,1,0:T(8,128)(2,1)S(1)}, f32[3,64,1536]{2,1,0:T(8,128)...) custom-call(s32[4]{0:T(128)S(1)} %pad_add_fusion.meta, ...), custom_call_target="tpu_custom_call", output_to_operand_aliasing={{2}: (5, {}), {3}: (6, {}), {4}: (7, {}), {5}: (8, {})} | custom-call | tf_op jit(solution)/shard_map/layer_turn/pallas_call | solution.py:127
  211.9 1.9 collective-permute-start.10
  214.0 3.8 settle.27
  217.8 3.0 collective-permute-done.10.g_ref
  220.7 3.6 layer_backward.7
  224.3 1.9 collective-permute-start.11
  226.4 4.2 %settle.28 = (bf16[1536,1536]{1,0:T(8,128)(2,1)S(1)}, bf16[1536,1536]{1,0:T(8,128)(2,1)S(1)}) custom-call(bf16[1536,1536]{1,0:T(8,128)(2,1)} %all-gather.6.cloned.1.call-done.refs_0_, bf16[1536,1536]{1,0:T(8,128)(2,1)} %collective-permute-done.refs_0_.refs_1_, bf16[64,1536]{1,0:T(8,128)(2,1)S(1)} %get-tuple-element.146.refs_2_), custom_call_target="tpu_custom_call" | custom-call | bytes 37748736 | tf_op jit(solution)/shard_map/settle/pallas_call | solution.py:45
  230.5 2.6 collective-permute-done.11.g_ref
  233.1 3.7 layer_backward.8
  236.8 11.5 %all-gather.8.cloned.1.call-done = bf16[6,64,1536]{2,1,0:T(8,128)(2,1)} async-done(((bf16[2,64,1536]{2,1,0:T(8,128)(2,1)}), bf16[6,64,1536]{2,1,0:T(8,128)(2,1)}) %all-gather.8.cloned.1.call-update) | async-done | bytes 1179664 | tf_op jit(solution)/shard_map/all_gather | solution.py:210
  248.3 2.4 collective-permute-start.12
  250.9 3.8 settle.29
  254.7 3.2 collective-permute-done.12.g_ref
  257.8 3.7 layer_backward.9
  261.5 2.1 collective-permute-start.13
  263.8 3.8 settle.30
  267.6 2.7 collective-permute-done.13.g_ref
  270.3 3.7 layer_backward.10
  274.0 1.9 collective-permute-start.14
  276.0 4.0 %settle.31 = (bf16[1536,1536]{1,0:T(8,128)(2,1)S(1)}, bf16[1536,1536]{1,0:T(8,128)(2,1)S(1)}) custom-call(bf16[1536,1536]{1,0:T(8,128)(2,1)} %all-gather.6.cloned.1.call-done.refs_0_, bf16[1536,1536]{1,0:T(8,128)(2,1)} %collective-permute-done.refs_0_.refs_1_, bf16[64,1536]{1,0:T(8,128)(2,1)S(1)} %get-tuple-element.160.refs_2_), custom_call_target="tpu_custom_call" | custom-call | bytes 37748736 | tf_op jit(solution)/shard_map/settle/pallas_call | solution.py:45
  280.0 2.8 collective-permute-done.14.g_ref
  282.8 3.7 layer_backward.11
  286.4 1.9 collective-permute-start.15
  288.4 4.0 %settle.32 = (bf16[1536,1536]{1,0:T(8,128)(2,1)S(1)}, bf16[1536,1536]{1,0:T(8,128)(2,1)S(1)}) custom-call(bf16[1536,1536]{1,0:T(8,128)(2,1)} %all-gather.6.cloned.1.call-done.refs_0_, bf16[1536,1536]{1,0:T(8,128)(2,1)} %collective-permute-done.refs_0_.refs_1_, bf16[64,1536]{1,0:T(8,128)(2,1)S(1)} %get-tuple-element.164.refs_2_), custom_call_target="tpu_custom_call" | custom-call | bytes 37748736 | tf_op jit(solution)/shard_map/settle/pallas_call | solution.py:45
  292.4 2.8 collective-permute-done.15.g_ref
  295.2 3.7 layer_backward.12
  298.9 1.9 collective-permute-start.16
  300.9 3.9 %settle.33 = (bf16[1536,1536]{1,0:T(8,128)(2,1)S(1)}, bf16[1536,1536]{1,0:T(8,128)(2,1)S(1)}) custom-call(bf16[1536,1536]{1,0:T(8,128)(2,1)} %all-gather.6.cloned.1.call-done.refs_0_, bf16[1536,1536]{1,0:T(8,128)(2,1)} %collective-permute-done.refs_0_.refs_1_, bf16[64,1536]{1,0:T(8,128)(2,1)S(1)} %get-tuple-element.168.refs_2_), custom_call_target="tpu_custom_call" | custom-call | bytes 37748736 | tf_op jit(solution)/shard_map/settle/pallas_call | solution.py:45
  304.8 2.8 collective-permute-done.16.g_ref
  307.7 4.4 %layer_backward.13 = (bf16[64,1536]{1,0:T(8,128)(2,1)}, bf16[3,64,1536]{2,1,0:T(8,128)(2,1)S(1)}) custom-call(s32[4]{0:T(128)S(1)} %pad_add_fusion.11.meta, bf16[64,1536]{1,0:T(8,128)(2,1)S(1)} %collective-permute-done.16.g_ref, bf16[1536,1536]{1,0:T(8,128)(2,1)S(1)} %get-tuple-element.169.own_ref, ...), custom_call_target="tpu_custom_call", output_to_operand_aliasing={{1}: (6, {})} | custom-call | tf_op jit(solution)/shard_map/layer_backward/pallas_call | solution.py:127
  313.7 5.7 %all-to-all-start.1 = ((bf16[24,128,64]{1,2,0:T(8,128)(2,1)}), bf16[24,128,64]{1,2,0:T(8,128)(2,1)S(1)}, u32[]{:S(2)}, u32[]{:S(2)}) async-start(bf16[24,128,64]{1,2,0:T(8,128)(2,1)} %copy.46), calls=%async_computation.1 | async-start | bytes 786432 | tf_op jit(solution)/shard_map/all_to_all | solution.py:216
  319.4 11.7 %all-to-all-done.1 = bf16[24,128,64]{1,2,0:T(8,128)(2,1)S(1)} async-done(((bf16[24,128,64]{1,2,0:T(8,128)(2,1)}), bf16[24,128,64]{1,2,0:T(8,128)(2,1)S(1)}, u32[]{:S(2)}, u32[]{:S(2)}) %all-to-all-start.1) | async-done | bytes 393248 | tf_op jit(solution)/shard_map/all_to_all | solution.py:216
  332.8 6.4 %convolution_convert_fusion = bf16[1536,128]{1,0:T(8,128)(2,1)S(1)} fusion(bf16[3072,1536]{1,0:T(8,128)(2,1)} %bitcast.76, bf16[3072,64]{0,1:T(8,128)(2,1)S(1)} %concatenate.13, bf16[3072,64]{0,1:T(8,128)(2,1)S(1)} %copy_bitcast_fusion), kind=kOutput, calls=%fused_computation | convolution fusion | flops 1209729024 | bytes 10616832 | tf_op jit(solution)/shard_map/dot_general | solution.py:219
  339.2 29.5 %all_to_all.28 = bf16[4,384,128]{2,1,0:T(8,128)(2,1)S(1)} all-to-all(bf16[4,384,128]{2,1,0:T(8,128)(2,1)S(1)} %bitcast.73), channel_id=1, replica_groups=mesh['section'=8,'zh'=4,'zl'=3,'x'=4,'core'=2] {'zh'}, dimensions={0} | all-to-all | bytes 786432 | tf_op jit(solution)/shard_map/all_to_all | solution.py:222
  368.7 11.4 %all_to_all.29 = f32[24,16,128]{2,1,0:T(8,128)S(1)} all-to-all(f32[24,16,128]{2,1,0:T(8,128)S(1)} %bitcast.72), channel_id=1, replica_groups=mesh['section'=8,'zh'=4,'zl'=3,'x'=4,'core'=2] {'zl','x','core'}, dimensions={0} | all-to-all | bytes 393216 | tf_op jit(solution)/shard_map/all_to_all | solution.py:224
  (69 shorter events, 16.4 us)
Async XLA Ops:
  6.5 91.1 %copy-start = (bf16[128,1536]{1,0:T(8,128)(2,1)S(1)}, bf16[128,1536]{1,0:T(8,128)(2,1)}, u32[]{:S(2)}) copy-start(bf16[128,1536]{1,0:T(8,128)(2,1)} %param.8) | copy-start | bytes 1179652
  6.5 88.5 %all-gather.6.cloned.1.call-start = ((), (), s32[]{:S(2)}) async-start(), calls=%async_computation.4 | async-start | bytes 5111808 | tf_op jit(solution)/shard_map/all_gather | solution.py:158
  20.7 227.6 %all-gather.8.cloned.1.call-start = ((), (), s32[]{:S(2)}) async-start(), calls=%async_computation.5 | async-start | bytes 1572864 | tf_op jit(solution)/shard_map/all_gather | solution.py:210
  95.0 10.1 %collective-permute-start = (bf16[1536,1536]{1,0:T(8,128)(2,1)}, bf16[1536,1536]{1,0:T(8,128)(2,1)}, u32[]{:S(2)}, u32[]{:S(2)}) collective-permute-start(bf16[1536,1536]{1,0:T(8,128)(2,1)} %all-gather.6.cloned.1.call-done.refs_0_), channel_id=1, source_target_pairs={{0,1},{1,0},{2,3},{3,2},{4,5},{5,4},{6,7},{7,6},{8,9},{9,8},{10,11... | collective-permute-start | bytes 14155784 | tf_op jit(solution)/shard_map/ppermute | solution.py:159
  110.2 9.1 %collective-permute-start.1 = (bf16[64,1536]{1,0:T(8,128)(2,1)S(1)}, bf16[64,1536]{1,0:T(8,128)(2,1)S(1)}, u32[]{:S(2)}, u32[]{:S(2)}) collective-permute-start(bf16[64,1536]{1,0:T(8,128)(2,1)S(1)} %get-tuple-element.89.refs_2_), channel_id=1, source_target_pairs={{0,96},{96,192},{192,288},{288,384},{384,480},{480,576},{576,672},... | collective-permute-start | bytes 589832 | tf_op jit(solution)/shard_map/ppermute | solution.py:206
  121.8 9.5 %collective-permute-start.2 = (bf16[64,1536]{1,0:T(8,128)(2,1)S(1)}, bf16[64,1536]{1,0:T(8,128)(2,1)S(1)}, u32[]{:S(2)}, u32[]{:S(2)}) collective-permute-start(bf16[64,1536]{1,0:T(8,128)(2,1)S(1)} %get-tuple-element.95.refs_2_), channel_id=1, source_target_pairs={{0,96},{96,192},{192,288},{288,384},{384,480},{480,576},{576,672},... | collective-permute-start | bytes 589832 | tf_op jit(solution)/shard_map/ppermute | solution.py:206
  133.8 9.2 %collective-permute-start.3 = (bf16[64,1536]{1,0:T(8,128)(2,1)S(1)}, bf16[64,1536]{1,0:T(8,128)(2,1)S(1)}, u32[]{:S(2)}, u32[]{:S(2)}) collective-permute-start(bf16[64,1536]{1,0:T(8,128)(2,1)S(1)} %get-tuple-element.101.refs_2_), channel_id=1, source_target_pairs={{0,96},{96,192},{192,288},{288,384},{384,480},{480,576},{576,672},... | collective-permute-start | bytes 589832 | tf_op jit(solution)/shard_map/ppermute | solution.py:206
  145.4 8.8 %collective-permute-start.4 = (bf16[64,1536]{1,0:T(8,128)(2,1)S(1)}, bf16[64,1536]{1,0:T(8,128)(2,1)S(1)}, u32[]{:S(2)}, u32[]{:S(2)}) collective-permute-start(bf16[64,1536]{1,0:T(8,128)(2,1)S(1)} %get-tuple-element.107.refs_2_), channel_id=1, source_target_pairs={{0,96},{96,192},{192,288},{288,384},{384,480},{480,576},{576,672},... | collective-permute-start | bytes 589832 | tf_op jit(solution)/shard_map/ppermute | solution.py:206
  156.6 8.8 %collective-permute-start.5 = (bf16[64,1536]{1,0:T(8,128)(2,1)S(1)}, bf16[64,1536]{1,0:T(8,128)(2,1)S(1)}, u32[]{:S(2)}, u32[]{:S(2)}) collective-permute-start(bf16[64,1536]{1,0:T(8,128)(2,1)S(1)} %get-tuple-element.113.refs_2_), channel_id=1, source_target_pairs={{0,96},{96,192},{192,288},{288,384},{384,480},{480,576},{576,672},... | collective-permute-start | bytes 589832 | tf_op jit(solution)/shard_map/ppermute | solution.py:206
  167.9 8.8 %collective-permute-start.6 = (bf16[64,1536]{1,0:T(8,128)(2,1)S(1)}, bf16[64,1536]{1,0:T(8,128)(2,1)S(1)}, u32[]{:S(2)}, u32[]{:S(2)}) collective-permute-start(bf16[64,1536]{1,0:T(8,128)(2,1)S(1)} %get-tuple-element.119.refs_2_), channel_id=1, source_target_pairs={{0,96},{96,192},{192,288},{288,384},{384,480},{480,576},{576,672},... | collective-permute-start | bytes 589832 | tf_op jit(solution)/shard_map/ppermute | solution.py:206
  176.6 7.5 %copy-start.3 = (bf16[2,1,64,1536]{3,2,1,0:T(8,128)(2,1)S(1)}, bf16[2,1,64,1536]{3,2,1,0:T(8,128)(2,1)}, u32[]{:S(2)}) copy-start(bf16[2,1,64,1536]{3,2,1,0:T(8,128)(2,1)} %param.11) | copy-start | bytes 1179652
  179.1 9.0 %collective-permute-start.7 = (bf16[64,1536]{1,0:T(8,128)(2,1)S(1)}, bf16[64,1536]{1,0:T(8,128)(2,1)S(1)}, u32[]{:S(2)}, u32[]{:S(2)}) collective-permute-start(bf16[64,1536]{1,0:T(8,128)(2,1)S(1)} %get-tuple-element.125.refs_2_), channel_id=1, source_target_pairs={{0,96},{96,192},{192,288},{288,384},{384,480},{480,576},{576,672},... | collective-permute-start | bytes 589832 | tf_op jit(solution)/shard_map/ppermute | solution.py:206
  193.7 0.7 copy-start.2
  194.4 11.1 %collective-permute-start.9 = (bf16[64,1536]{1,0:T(8,128)(2,1)S(1)}, bf16[64,1536]{1,0:T(8,128)(2,1)S(1)}, u32[]{:S(2)}, u32[]{:S(2)}) collective-permute-start(bf16[64,1536]{1,0:T(8,128)(2,1)S(1)} %get-tuple-element.132.refs_2_), channel_id=1, source_target_pairs={{96,0},{192,96},{288,192},{384,288},{480,384},{576,480},{672,576},... | collective-permute-start | bytes 589832 | tf_op jit(solution)/shard_map/ppermute | solution.py:208
  196.4 9.1 %copy-start.4 = (bf16[2,1,64,1536]{3,2,1,0:T(8,128)(2,1)S(1)}, bf16[2,1,64,1536]{3,2,1,0:T(8,128)(2,1)}, u32[]{:S(2)}) copy-start(bf16[2,1,64,1536]{3,2,1,0:T(8,128)(2,1)} %param.11) | copy-start | bytes 1179652
  196.4 9.1 %collective-permute-start.8 = (bf16[64,1536]{1,0:T(8,128)(2,1)}, bf16[64,1536]{1,0:T(8,128)(2,1)S(1)}, u32[]{:S(2)}, u32[]{:S(2)}) collective-permute-start(bf16[64,1536]{1,0:T(8,128)(2,1)} %copy-done.2), channel_id=1, source_target_pairs={{0,96},{96,192},{192,288},{288,384},{384,480},{480,576},{576,672},... | collective-permute-start | bytes 589832 | tf_op jit(solution)/shard_map/ppermute | solution.py:206
  211.9 120.9 %all-gather.10.cloned.1.call-start = ((), (), s32[]{:S(2)}) async-start(), calls=%async_computation.6 | async-start | bytes 10616832 | tf_op jit(solution)/shard_map/all_gather | solution.py:202
  211.9 8.8 %collective-permute-start.10 = (bf16[64,1536]{1,0:T(8,128)(2,1)S(1)}, bf16[64,1536]{1,0:T(8,128)(2,1)S(1)}, u32[]{:S(2)}, u32[]{:S(2)}) collective-permute-start(bf16[64,1536]{1,0:T(8,128)(2,1)S(1)} %get-tuple-element.140.refs_2_), channel_id=1, source_target_pairs={{96,0},{192,96},{288,192},{384,288},{480,384},{576,480},{672,576},... | collective-permute-start | bytes 589832 | tf_op jit(solution)/shard_map/ppermute | solution.py:208
  224.3 8.8 %collective-permute-start.11 = (bf16[64,1536]{1,0:T(8,128)(2,1)S(1)}, bf16[64,1536]{1,0:T(8,128)(2,1)S(1)}, u32[]{:S(2)}, u32[]{:S(2)}) collective-permute-start(bf16[64,1536]{1,0:T(8,128)(2,1)S(1)} %get-tuple-element.146.refs_2_), channel_id=1, source_target_pairs={{96,0},{192,96},{288,192},{384,288},{480,384},{576,480},{672,576},... | collective-permute-start | bytes 589832 | tf_op jit(solution)/shard_map/ppermute | solution.py:208
  248.3 9.5 %collective-permute-start.12 = (bf16[64,1536]{1,0:T(8,128)(2,1)S(1)}, bf16[64,1536]{1,0:T(8,128)(2,1)S(1)}, u32[]{:S(2)}, u32[]{:S(2)}) collective-permute-start(bf16[64,1536]{1,0:T(8,128)(2,1)S(1)} %get-tuple-element.152.refs_2_), channel_id=1, source_target_pairs={{96,0},{192,96},{288,192},{384,288},{480,384},{576,480},{672,576},... | collective-permute-start | bytes 589832 | tf_op jit(solution)/shard_map/ppermute | solution.py:208
  261.5 8.8 %collective-permute-start.13 = (bf16[64,1536]{1,0:T(8,128)(2,1)S(1)}, bf16[64,1536]{1,0:T(8,128)(2,1)S(1)}, u32[]{:S(2)}, u32[]{:S(2)}) collective-permute-start(bf16[64,1536]{1,0:T(8,128)(2,1)S(1)} %get-tuple-element.156.refs_2_), channel_id=1, source_target_pairs={{96,0},{192,96},{288,192},{384,288},{480,384},{576,480},{672,576},... | collective-permute-start | bytes 589832 | tf_op jit(solution)/shard_map/ppermute | solution.py:208
  274.0 8.8 %collective-permute-start.14 = (bf16[64,1536]{1,0:T(8,128)(2,1)S(1)}, bf16[64,1536]{1,0:T(8,128)(2,1)S(1)}, u32[]{:S(2)}, u32[]{:S(2)}) collective-permute-start(bf16[64,1536]{1,0:T(8,128)(2,1)S(1)} %get-tuple-element.160.refs_2_), channel_id=1, source_target_pairs={{96,0},{192,96},{288,192},{384,288},{480,384},{576,480},{672,576},... | collective-permute-start | bytes 589832 | tf_op jit(solution)/shard_map/ppermute | solution.py:208
  286.4 8.8 %collective-permute-start.15 = (bf16[64,1536]{1,0:T(8,128)(2,1)S(1)}, bf16[64,1536]{1,0:T(8,128)(2,1)S(1)}, u32[]{:S(2)}, u32[]{:S(2)}) collective-permute-start(bf16[64,1536]{1,0:T(8,128)(2,1)S(1)} %get-tuple-element.164.refs_2_), channel_id=1, source_target_pairs={{96,0},{192,96},{288,192},{384,288},{480,384},{576,480},{672,576},... | collective-permute-start | bytes 589832 | tf_op jit(solution)/shard_map/ppermute | solution.py:208
  298.9 8.8 %collective-permute-start.16 = (bf16[64,1536]{1,0:T(8,128)(2,1)S(1)}, bf16[64,1536]{1,0:T(8,128)(2,1)S(1)}, u32[]{:S(2)}, u32[]{:S(2)}) collective-permute-start(bf16[64,1536]{1,0:T(8,128)(2,1)S(1)} %get-tuple-element.168.refs_2_), channel_id=1, source_target_pairs={{96,0},{192,96},{288,192},{384,288},{480,384},{576,480},{672,576},... | collective-permute-start | bytes 589832 | tf_op jit(solution)/shard_map/ppermute | solution.py:208
  313.7 17.5 %all-to-all-start.1 = ((bf16[24,128,64]{1,2,0:T(8,128)(2,1)}), bf16[24,128,64]{1,2,0:T(8,128)(2,1)S(1)}, u32[]{:S(2)}, u32[]{:S(2)}) async-start(bf16[24,128,64]{1,2,0:T(8,128)(2,1)} %copy.46), calls=%async_computation.1 | async-start | bytes 786432 | tf_op jit(solution)/shard_map/all_to_all | solution.py:216
  332.8 48.9 %copy-start.1 = (bf16[128,1536]{1,0:T(8,128)(2,1)S(1)}, bf16[128,1536]{1,0:T(8,128)(2,1)}, u32[]{:S(2)}) copy-start(bf16[128,1536]{1,0:T(8,128)(2,1)} %param.8) | copy-start | bytes 1179652
Sparse Core Ops, SparseCore 0:
  20.8 74.1 all-gather.5
  212.0 36.2 all-gather.7
  250.7 63.1 all-gather.9
